TPU v7x, 256 devices: a whole 4x4x8 slice. The times are simulated.
256 devices in a mesh: ctx: 16 (over z, x_hi), fsdp: 16 (over x_lo, y, core).
Axes of the slice: x: 4 (x_hi: 2, x_lo: 2; x = x_hi * 2 + x_lo), y: 4, z: 8, core: 2. Of those that a mesh axis runs over, the one named last changes fastest.
Arguments:
- out_grad: bfloat16 [2048, 8192], P('ctx', 'fsdp'), may hold values from -6 to 6
- out_weight: bfloat16 [8192, 8192], P('ctx', 'fsdp'), may hold values from -0.0625 to 0.0625
- projections: bfloat16 [3, 2048, 8192], P(None, 'ctx', 'fsdp'), may hold values from -6 to 6
- short_filters: float32 [3, 3, 8192], P(None, None, 'fsdp'), may hold values from -3 to 3
- residues: float32 [16, 8192], P(None, 'fsdp'), may hold values from -0.06 to 0.06
- decay_rates: float32 [16, 8192], P(None, 'fsdp'), may hold values from 4.8828126e-05 to 0.05
Outputs:
- grad_weight: bfloat16 [8192, 8192], P('ctx', 'fsdp')
- grad_projections: bfloat16 [3, 2048, 8192], P(None, 'ctx', 'fsdp')
- grad_short: float32 [3, 3, 8192], P(None, None, 'fsdp')
- grad_residues: float32 [16, 8192], P(None, 'fsdp')
- grad_rates: float32 [16, 8192], P(None, 'fsdp')
All inputs are finite; a program needn't handle non-finite values.
Results may differ from a plain program's by a relative error of at most 0.005.
Values may be sent and summed in bfloat16 or wider, within the bound.
No kernel may reach another device: no remote copies, remote signals or barrier semaphores. Data moves between devices by JAX's collectives and lax.ppermute only.
A program may use at most 128 MiB of HBM per device.

v0:
```python
import math

import jax
import jax.numpy as jnp
from jax import lax
from jax.sharding import PartitionSpec as P


def from_behind(block, axis, distance):
    devices = range(lax.axis_size(axis))
    route = [(i - distance, i) for i in devices if i - distance in devices]
    return lax.ppermute(block, axis, route)


def carried_in(array, axis, combine, identity, reverse):
    devices, index = (lax.axis_size(axis), lax.axis_index(axis))
    everything = jax.tree.map(lambda part: lax.all_gather(part, axis), array)
    start = jax.tree.map(
        lambda part, zero: jnp.broadcast_to(jnp.asarray(zero, part.dtype), part.shape),
        array,
        identity,
    )

    def lap(k, before):
        at = devices - 1 - k if reverse else k
        reached = at > index if reverse else at < index
        new = combine(before, jax.tree.map(lambda part: part[at], everything))
        return jax.tree.map(lambda a, b: jnp.where(reached, a, b), new, before)

    return lax.fori_loop(0, devices, lap, start)


def link(earlier, later):
    return (earlier[0] * later[0], later[0] * earlier[1] + later[1])


def local_scan(decay, values):
    length = values.shape[0]
    piece_len = math.gcd(length, 32)
    block_count = length // piece_len
    grouped = values.reshape((block_count, piece_len) + values.shape[1:])
    running = jnp.zeros((block_count,) + decay.shape, jnp.float32)
    outputs = []
    for offset in range(piece_len):
        running = decay * running + grouped[:, offset]
        outputs.append(running)
    inner = jnp.stack(outputs, axis=1)
    jump = jnp.power(decay, float(piece_len))

    def carry_step(carry, final):
        return (jump * carry + final, carry)

    _, entering = lax.scan(carry_step, jnp.zeros(decay.shape, jnp.float32), inner[:, -1])
    steps_in = jnp.arange(piece_len, dtype=jnp.float32) + 1.0
    rising = jnp.power(decay[None], steps_in[:, None, None])
    whole = inner + rising[None] * entering[:, None]
    return whole.reshape((length,) + decay.shape)


def on_device(out_grad, out_weight, projections, short_filters, residues, decay_rates):
    panels = lax.all_gather(out_grad, "fsdp", axis=1, tiled=True)
    length = out_grad.shape[0]
    columns = panels
    grad_y = jnp.dot(
        columns,
        lax.all_gather(out_weight, "ctx", axis=0, tiled=True),
        preferred_element_type=jnp.float32,
    )
    taps = short_filters.shape[1]
    margin = taps - 1
    before = from_behind(projections[:, length - margin :, :], "ctx", 1)
    extended = jnp.concatenate([before, projections], axis=1).astype(jnp.float32)
    branches = short_filters[:, 0, None, :] * extended[:, margin : margin + length, :]
    for offset in range(1, taps):
        branches = (
            branches
            + short_filters[:, offset, None, :]
            * extended[:, margin - offset : margin - offset + length, :]
        )
    q_branch, k_branch, v_branch = (branches[0], branches[1], branches[2])
    product_kv = k_branch * v_branch
    decay = jnp.exp(-decay_rates)
    block_decay = jnp.exp(-decay_rates * float(length))
    positions = jnp.arange(length, dtype=jnp.float32)
    states_local = local_scan(decay, product_kv[:, None, :])
    identity = (jnp.ones_like(decay), jnp.zeros_like(decay))
    state_in = carried_in((block_decay, states_local[-1]), "ctx", link, identity, False)[1]
    rising = jnp.exp(-decay_rates[None] * (positions + 1.0)[:, None, None])
    states = states_local + rising * state_in[None]
    long_out = jnp.sum(residues[None] * states, axis=1)
    y_rounded = (q_branch * long_out).astype(jnp.bfloat16)
    grad_long = grad_y * q_branch
    grad_q = grad_y * long_out
    flipped = jnp.flip(grad_long, axis=0)
    adjoint_local = jnp.flip(local_scan(decay, residues[None] * flipped[:, None, :]), axis=0)
    adjoint_in = carried_in((block_decay, adjoint_local[0]), "ctx", link, identity, True)[1]
    falling = jnp.exp(-decay_rates[None] * (float(length) - positions)[:, None, None])
    adjoint = adjoint_local + falling * adjoint_in[None]
    grad_kv = jnp.sum(adjoint, axis=1)
    grad_res_part = jnp.sum(grad_long[:, None, :] * states, axis=0)
    previous = jnp.concatenate([state_in[None], states[:-1]], axis=0)
    grad_rate_part = -decay * jnp.sum(adjoint * previous, axis=0)
    grad_branches = jnp.stack([grad_q, grad_kv * v_branch, grad_kv * k_branch])
    after = from_behind(grad_branches[:, :margin, :], "ctx", -1)
    extended_back = jnp.concatenate([grad_branches, after], axis=1)
    grad_raw = short_filters[:, 0, None, :] * extended_back[:, 0:length, :]
    filter_terms = [jnp.sum(grad_branches * extended[:, margin : margin + length, :], axis=1)]
    for offset in range(1, taps):
        grad_raw = (
            grad_raw
            + short_filters[:, offset, None, :] * extended_back[:, offset : offset + length, :]
        )
        filter_terms.append(
            jnp.sum(
                grad_branches * extended[:, margin - offset : margin - offset + length, :], axis=1
            )
        )
    filter_part = jnp.stack(filter_terms, axis=1)
    grad_short, grad_res, grad_rate = lax.psum((filter_part, grad_res_part, grad_rate_part), "ctx")
    columns = panels
    grad_weight = lax.psum_scatter(
        lax.dot_general(
            columns, y_rounded, (((0,), (0,)), ((), ())), preferred_element_type=jnp.float32
        ),
        "ctx",
        scatter_dimension=0,
        tiled=True,
    )
    return (
        grad_weight.astype(jnp.bfloat16),
        grad_raw.astype(jnp.bfloat16),
        grad_short,
        grad_res,
        grad_rate,
    )


def solution(mesh):
    placed = (
        P("ctx", "fsdp"),
        P("ctx", "fsdp"),
        P(None, "ctx", "fsdp"),
        P(None, None, "fsdp"),
        P(None, "fsdp"),
        P(None, "fsdp"),
    )
    return jax.shard_map(
        on_device,
        mesh=mesh,
        in_specs=placed,
        out_specs=(
            P("ctx", "fsdp"),
            P(None, "ctx", "fsdp"),
            P(None, None, "fsdp"),
            P(None, "fsdp"),
            P(None, "fsdp"),
        ),
        check_vma=False,
    )
```

profile of v0, /device:TPU:16, one launch (start us, length us, event | category | flops | bytes accessed | tf_op | source)
XLA Modules:
  0.0 869.9 jit_solution(4104952560245108531)
XLA Ops:
  9.4 4.9 collective-permute-start
  17.9 45.8 %all-gather = f32[256,512]{1,0:T(8,128)} all-gather(f32[16,512]{1,0:T(8,128)S(1)} %get-tuple-element.508), channel_id=2, replica_groups=mesh['ctx'=16,'fsdp'=16] {'ctx'}, dimensions={0}, use_global_device_ids=true | all-gather | bytes 557056 | tf_op jit(solution)/shard_map/all_gather | solution.py:17
  63.7 1.8 broadcast_power_fusion
  74.4 113.8 %all-gather.6.cloned.1.call-done = bf16[8192,512]{1,0:T(8,128)(2,1)} async-done(((bf16[512,512]{1,0:T(8,128)(2,1)}), bf16[8192,512]{1,0:T(8,128)(2,1)}) %all-gather.6.cloned.1.call-update) | async-done | bytes 8388624 | tf_op jit(solution)/shard_map/all_gather | solution.py:66
  188.1 5.3 fusion.8
  239.0 1.7 constant_dynamic-update-slice_fusion.37
  247.3 1.7 constant_dynamic-update-slice_fusion.32
  254.6 1.7 constant_dynamic-update-slice_fusion.31
  265.0 5.6 while.58
  270.6 7.2 multiply_add_fusion.1
  279.8 2.0 copy-done.5
  281.9 40.0 %all_gather.22 = f32[16,16,512]{2,1,0:T(8,128)S(1)} all-gather(f32[1,16,512]{2,1,0:T(8,128)S(1)} %slice.365), channel_id=1, replica_groups=mesh['ctx'=16,'fsdp'=16] {'ctx'}, dimensions={0}, use_global_device_ids=true | all-gather | bytes 557056 | tf_op jit(solution)/shard_map/all_gather | solution.py:17
  321.9 12.7 %while.57 = (s32[]{:T(128)}, f32[16,512]{1,0:T(8,128)S(1)}, s32[]{:T(128)}, f32[16,16,512]{2,1,0:T(8,128)}, f32[16,16,512]{2,1,0:T(8,128)S(1)}, /*index=5*/s32[]{:T(128)}, s32[]{:T(128)}) while((s32[]{:T(128)}, f32[16,512]{1,0:T(8,128)S(1)}, s32[]{:T(128)}, f32[16,16,512]{2,1,0:T(8,128)}, f32[16,16,512]{2,1,0:T(8,128)S(1)}, ...), condition=%wide.region_3.4_spmd.clone, body=%wide.region_2.3_spmd.clone.sunk | while | flops 32772 | bytes 131173 | solution.py:30
  334.6 2.6 copy.25
  337.3 2.1 copy-done.3
  339.4 40.3 %all_gather.25 = f32[16,16,512]{2,1,0:T(8,128)S(1)} all-gather(f32[1,16,512]{2,1,0:T(8,128)S(1)} %slice.398), channel_id=1, replica_groups=mesh['ctx'=16,'fsdp'=16] {'ctx'}, dimensions={0}, use_global_device_ids=true | all-gather | bytes 557056 | tf_op jit(solution)/shard_map/all_gather | solution.py:17
  379.6 12.8 %while.59 = (s32[]{:T(128)}, f32[16,512]{1,0:T(8,128)S(1)}, s32[]{:T(128)}, f32[16,16,512]{2,1,0:T(8,128)}, f32[16,16,512]{2,1,0:T(8,128)S(1)}, /*index=5*/s32[]{:T(128)}, s32[]{:T(128)}, s32[]{:T(128)}, s32[]{:T(128)}) while((s32[]{:T(128)}, f32[16,512]{1,0:T(8,128)S(1)}, s32[]{:T(128)}, f32[16,16,512]{2,1,0:T(8,128)}, ...), condition=%wide.region_9.10_spmd.clone, body=%wide.region_8.9_spmd.clone.sunk | while | flops 32776 | bytes 131235 | solution.py:30
  392.5 3.1 slice_add_fusion
  395.9 2.3 fusion.2
  398.5 2.5 multiply_reduce_fusion
  403.3 5.2 collective-permute-done.1
  410.6 8.2 convolution_bitcast_fusion
  418.8 149.0 %all-reduce.3.cloned.1.call-done = (f32[3,3,512]{2,0,1:T(4,128)}, f32[16,512]{1,0:T(8,128)}, f32[16,512]{1,0:T(8,128)}) async-done(((f32[3,3,512]{2,0,1:T(4,128)}, f32[16,512]{1,0:T(8,128)}, f32[16,512]{1,0:T(8,128)}), (f32[3,3,512]{2,0,1:T(4,128)}, f32[16,512]{1,0:T(8,128)}, f32[16,512]{1,0:T(8,128)})) %all-reduce.3.cloned.1.call-update) | async-done | bytes 83984 | tf_op jit(solution)/shard_map/psum | solution.py:119
  569.1 289.2 %reduce-scatter.2.cloned.1.call-done = f32[512,512]{0,1:T(8,128)} async-done(((f32[8192,512]{0,1:T(8,128)}), f32[512,512]{0,1:T(8,128)}) %reduce-scatter.2.cloned.1.call-update) | async-done | bytes 1048592 | tf_op jit(solution)/shard_map/reduce_scatter | solution.py:121
  (296 shorter events, 124.1 us)
Async XLA Ops:
  7.2 66.6 %all-gather.4.cloned.1.call-start = ((), (), s32[]{:S(2)}) async-start(), calls=%async_computation.1 | async-start | bytes 2228224 | tf_op jit(solution)/shard_map/all_gather | solution.py:61
  7.9 180.2 %all-gather.6.cloned.1.call-start = ((), (), s32[]{:S(2)}) async-start(), calls=%async_computation.3 | async-start | bytes 8912896 | tf_op jit(solution)/shard_map/all_gather | solution.py:66
  8.6 559.1 %all-reduce.3.cloned.1.call-start = ((), (), s32[]{:S(2)}) async-start(), calls=%async_computation.4 | async-start | bytes 180224 | tf_op jit(solution)/shard_map/psum | solution.py:119
  9.4 56.6 %collective-permute-start = (bf16[3,2,512]{2,1,0:T(2,128)(2,1)S(1)}, bf16[3,2,512]{2,1,0:T(2,128)(2,1)S(1)}, u32[]{:S(2)}, u32[]{:S(2)}) collective-permute-start(bf16[3,2,512]{2,1,0:T(2,128)(2,1)S(1)} %slice.248), channel_id=1, source_target_pairs={{0,16},{16,32},{32,48},{48,64},{64,80},{80,96},{96,112},{112,128},... | collective-permute-start | bytes 18440 | tf_op jit(solution)/shard_map/ppermute | solution.py:12
  16.5 51.1 %copy-start.40 = (f32[3,512]{1,0:T(4,128)}, f32[3,512]{1,0:T(4,128)S(1)}, u32[]{:S(2)}) copy-start(f32[3,512]{1,0:T(4,128)S(1)} %get-tuple-element.514) | copy-start | bytes 18436
  16.5 51.1 %copy-start.42 = (f32[3,512]{1,0:T(4,128)}, f32[3,512]{1,0:T(4,128)S(1)}, u32[]{:S(2)}) copy-start(f32[3,512]{1,0:T(4,128)S(1)} %get-tuple-element.515) | copy-start | bytes 18436
  73.7 122.1 %copy-start.33 = (f32[16,512]{1,0:T(8,128)S(1)}, f32[16,512]{1,0:T(8,128)}, u32[]{:S(2)}) copy-start(f32[16,512]{1,0:T(8,128)} %param.18) | copy-start | bytes 98308
  222.8 24.5 %copy-start.8 = (f32[4,1,1,512]{3,0,1,2:T(4,128)S(1)}, f32[4,1,1,512]{3,0,1,2:T(4,128)}, u32[]{:S(2)}) copy-start(f32[4,1,1,512]{3,0,1,2:T(4,128)} %copy-done.7) | copy-start | bytes 24580
  224.4 24.6 %copy-start.14 = (f32[4,1,1,512]{3,0,1,2:T(4,128)S(1)}, f32[4,1,1,512]{3,0,1,2:T(4,128)}, u32[]{:S(2)}) copy-start(f32[4,1,1,512]{3,0,1,2:T(4,128)} %copy-done.13) | copy-start | bytes 24580
  226.0 23.8 %copy-start.20 = (f32[4,1,1,512]{3,0,1,2:T(4,128)S(1)}, f32[4,1,1,512]{3,0,1,2:T(4,128)}, u32[]{:S(2)}) copy-start(f32[4,1,1,512]{3,0,1,2:T(4,128)} %copy-done.19) | copy-start | bytes 24580
  226.0 24.6 %copy-start.24 = (f32[4,1,1,512]{3,0,1,2:T(4,128)S(1)}, f32[4,1,1,512]{3,0,1,2:T(4,128)}, u32[]{:S(2)}) copy-start(f32[4,1,1,512]{3,0,1,2:T(4,128)} %copy-done.23) | copy-start | bytes 24580
  227.7 23.7 %copy-start.28 = (f32[4,1,1,512]{3,0,1,2:T(4,128)S(1)}, f32[4,1,1,512]{3,0,1,2:T(4,128)}, u32[]{:S(2)}) copy-start(f32[4,1,1,512]{3,0,1,2:T(4,128)} %copy-done.27) | copy-start | bytes 24580
  229.3 22.9 %copy-start.30 = (f32[4,1,1,512]{3,0,1,2:T(4,128)S(1)}, f32[4,1,1,512]{3,0,1,2:T(4,128)}, u32[]{:S(2)}) copy-start(f32[4,1,1,512]{3,0,1,2:T(4,128)} %copy-done.29) | copy-start | bytes 24580
  229.3 23.7 %copy-start.36 = (f32[4,1,1,512]{3,0,1,2:T(4,128)S(1)}, f32[4,1,1,512]{3,0,1,2:T(4,128)}, u32[]{:S(2)}) copy-start(f32[4,1,1,512]{3,0,1,2:T(4,128)} %copy-done.35) | copy-start | bytes 24580
  230.9 22.8 %copy-start.47 = (f32[4,1,1,512]{3,0,1,2:T(4,128)S(1)}, f32[4,1,1,512]{3,0,1,2:T(4,128)}, u32[]{:S(2)}) copy-start(f32[4,1,1,512]{3,0,1,2:T(4,128)} %copy-done.46) | copy-start | bytes 24580
  237.4 20.9 %copy-start.10 = (f32[4,1,1,512]{3,0,1,2:T(4,128)S(1)}, f32[4,1,1,512]{3,0,1,2:T(4,128)}, u32[]{:S(2)}) copy-start(f32[4,1,1,512]{3,0,1,2:T(4,128)} %copy-done.9) | copy-start | bytes 24580
  239.0 20.1 %copy-start.12 = (f32[4,1,1,512]{3,0,1,2:T(4,128)S(1)}, f32[4,1,1,512]{3,0,1,2:T(4,128)}, u32[]{:S(2)}) copy-start(f32[4,1,1,512]{3,0,1,2:T(4,128)} %copy-done.11) | copy-start | bytes 24580
  239.0 20.8 %copy-start.18 = (f32[4,1,1,512]{3,0,1,2:T(4,128)S(1)}, f32[4,1,1,512]{3,0,1,2:T(4,128)}, u32[]{:S(2)}) copy-start(f32[4,1,1,512]{3,0,1,2:T(4,128)} %copy-done.17) | copy-start | bytes 24580
  240.7 19.8 %copy-start.22 = (f32[4,1,1,512]{3,0,1,2:T(4,128)S(1)}, f32[4,1,1,512]{3,0,1,2:T(4,128)}, u32[]{:S(2)}) copy-start(f32[4,1,1,512]{3,0,1,2:T(4,128)} %copy-done.21) | copy-start | bytes 24580
  242.3 19.7 %copy-start.32 = (f32[4,1,1,512]{3,0,1,2:T(4,128)S(1)}, f32[4,1,1,512]{3,0,1,2:T(4,128)}, u32[]{:S(2)}) copy-start(f32[4,1,1,512]{3,0,1,2:T(4,128)} %copy-done.31) | copy-start | bytes 24580
  334.6 57.9 %copy-start.15 = (f32[16,512]{1,0:T(8,128)S(1)}, f32[16,512]{1,0:T(8,128)}, u32[]{:S(2)}) copy-start(f32[16,512]{1,0:T(8,128)} %get-tuple-element.504) | copy-start | bytes 98308
  334.6 57.9 %copy-start.51 = (f32[128]{0:T(128)S(1)}, f32[128]{0:T(128)}, u32[]{:S(2)}) copy-start(f32[128]{0:T(128)} %iota_add_fusion) | copy-start | bytes 1540
  401.3 7.2 collective-permute-start.1
  410.5 447.8 %reduce-scatter.2.cloned.1.call-start = ((), (), s32[]{:S(2)}) async-start(), calls=%async_computation.2 | async-start | bytes 17825792 | tf_op jit(solution)/shard_map/reduce_scatter | solution.py:121
  (35 other events, 220.5 us)
Sparse Core Ops, SparseCore 0:
  9.8 39.3 all-gather.3
  51.8 136.2 all-gather.5
  410.6 157.0 all-reduce.2
  571.7 286.5 reduce-scatter.1
where the time goes:
time: 874 us; the launch traced here: 870 us
  waiting for transfers between devices  559 us (64%)
  other arithmetic  127 us (15%)
  blocking collectives  126 us (14%)
  local copies, waits for them, and re-layouts  21.9 us (3%)
  between operations  14.8 us (2%)
  matrix products  13.4 us (2%)
    reduce_scatter x1, waiting for transfers between devices, on_device(): lax.psum_scatter(lax.dot_general(columns, y_rounded, (((0,), (0,)), ((),...  289 us
    psum x1, waiting for transfers between devices, on_device(): lax.psum((filter_part, grad_res_part, grad_rate_part), 'ctx')  149 us
    all_gather x3, blocking collectives, carried_in(): everything = jax.tree.map(lambda part: lax.all_gather(part, axis), array)  126 us
    all_gather x1, waiting for transfers between devices, on_device(): lax.all_gather(out_weight, 'ctx', axis=0, tiled=True)  114 us
    unnamed x62, other arithmetic  68.5 us
    select_n x32, other arithmetic, lap(): return jax.tree.map(lambda a, b: jnp.where(reached, a, b), new, before)  24.7 us
  transfers between devices with their start and end apart: 6, of which 4 were waited for; matrix products, arithmetic and copies ran while one was open for 3% of the time, Pallas kernels for 0%

commit v1 on v0

v1 whole, which is shorter than its diff:
```python
import jax
import jax.numpy as jnp
from jax import lax
from jax.experimental import pallas as pl
from jax.experimental.pallas import tpu as pltpu
from jax.sharding import Mesh
from jax.sharding import PartitionSpec as P

F32 = jnp.float32
BF16 = jnp.bfloat16
CTX = ("z", "xh")
FSDP = ("xl", "y", "core")
SUB = 32
NM = 16
STEPS = 32
NK = 16
ROWS = STEPS * NK
VMEM = pl.BlockSpec(memory_space=pltpu.VMEM)
RES, RATE, TAP = 0, 16, 32
PARAMS = pltpu.CompilerParams(vmem_limit_bytes=48 * 2**20)


def lane_group(shape):
    return lax.broadcasted_iota(jnp.int32, shape, len(shape) - 1) // SUB


def swap4(parts):
    group = lane_group(parts[0].shape)
    outs = []
    for r in range(4):
        total = None
        for q in range(4):
            turn = (SUB * (q - r)) % 128
            moved = parts[q] if turn == 0 else pltpu.roll(parts[q], turn, 1)
            total = moved if total is None else jnp.where(group == q, moved, total)
        outs.append(total)
    return outs


def shift_blocks(values, blocks, reverse=False):
    rows = values.shape[0]
    row = lax.broadcasted_iota(jnp.int32, values.shape, 0) % NK
    group = lane_group(values.shape)
    if blocks >= 4:
        by = blocks // 4
        if reverse:
            return jnp.where(row < NK - by, pltpu.roll(values, rows - by, 0), 0.0)
        return jnp.where(row >= by, pltpu.roll(values, by, 0), 0.0)
    if reverse:
        turned = pltpu.roll(values, 128 - SUB * blocks, 1)
        over = jnp.where(row < NK - 1, pltpu.roll(turned, rows - 1, 0), 0.0)
        return jnp.where(group >= 4 - blocks, over, turned)
    turned = pltpu.roll(values, SUB * blocks, 1)
    over = jnp.where(row >= 1, pltpu.roll(turned, 1, 0), 0.0)
    return jnp.where(group < blocks, over, turned)


def pack_kernel(x_ref, o_ref):
    for p in range(3):
        for g in range(4):
            parts = [
                x_ref[p, q * STEPS : (q + 1) * STEPS, g * 128 : (g + 1) * 128].astype(F32)
                for q in range(4)
            ]
            for r, out in enumerate(swap4(parts)):
                o_ref[4 * g + r, p * STEPS : (p + 1) * STEPS, :] = out.astype(BF16)


def prepare(x_ref, prm_ref, wide, x_ext, branch):
    wide[...] = x_ref[...].reshape(NK * 96, 128).astype(F32)
    for p in range(3):
        for t in range(STEPS):
            x_ext[p, (t + 2) * NK : (t + 3) * NK, :] = wide[pl.ds(p * STEPS + t, NK, stride=96), :]
        for back in range(2):
            x_ext[p, back * NK : (back + 1) * NK, :] = shift_blocks(
                x_ext[p, (STEPS + back) * NK : (STEPS + back + 1) * NK, :], 1
            )
        total = None
        for j in range(3):
            tap = prm_ref[TAP + 3 * p + j : TAP + 3 * p + j + 1, :]
            term = tap * x_ext[p, (2 - j) * NK : (2 - j) * NK + ROWS, :]
            total = term if total is None else total + term
        branch[p] = total


def spread(prm_ref, first, out):
    for n in range(NM):
        out[n * NK : (n + 1) * NK, :] = jnp.broadcast_to(
            prm_ref[first + n : first + n + 1, :], (NK, 128)
        )


def ends(source, decay8, out, reverse):
    for v in range(2):

        def step(i, state):
            t = STEPS - 1 - i if reverse else i
            value = source[pl.ds(pl.multiple_of(t * NK + v * 8, 8), 8), :]
            return tuple(decay8[n] * state[n] + value for n in range(NM))

        state = lax.fori_loop(
            0, STEPS, step, tuple(jnp.zeros((8, 128), F32) for _ in range(NM)), unroll=4
        )
        for n in range(NM):
            out[n * NK + v * 8 : n * NK + v * 8 + 8, :] = state[n]


def entering(ends_ref, rates, reverse):
    total = ends_ref[...]
    for log in range(6):
        blocks = 2**log
        power = jnp.exp(rates[...] * (-float(STEPS * blocks)))
        total = total + power * shift_blocks(total, blocks, reverse)
    return shift_blocks(total, 1, reverse)


def decays(prm_ref):
    return [
        jnp.exp(-jnp.broadcast_to(prm_ref[RATE + n : RATE + n + 1, :], (8, 128)))
        for n in range(NM)
    ]


def weights(prm_ref):
    return [jnp.broadcast_to(prm_ref[RES + n : RES + n + 1, :], (8, 128)) for n in range(NM)]


def forward_kernel(h_ref, x_ref, prm_ref, keep_ref, send_ref, in_ref, wide, x_ext, branch, kv, rates, tails, y):
    prepare(x_ref, prm_ref, wide, x_ext, branch)
    kv[...] = branch[1] * branch[2]
    spread(prm_ref, RATE, rates)
    decay8 = decays(prm_ref)
    ends(kv, decay8, tails, False)
    in_ref[...] = entering(tails, rates, False)
    weight8 = weights(prm_ref)
    for v in range(2):

        def step(t, state):
            at = pl.ds(pl.multiple_of(t * NK + v * 8, 8), 8)
            value = kv[at, :]
            state = tuple(decay8[n] * state[n] + value for n in range(NM))
            terms = [weight8[n] * state[n] for n in range(NM)]
            while len(terms) > 1:
                terms = [a + b for a, b in zip(terms[::2], terms[1::2])]
            y[at, :] = branch[0, at, :] * terms[0]
            return state

        lax.fori_loop(
            0,
            STEPS,
            step,
            tuple(in_ref[n * NK + v * 8 : n * NK + v * 8 + 8, :] for n in range(NM)),
            unroll=2,
        )
    h = h_ref[0]
    for k in range(8):
        keep_ref[k] = y[pl.ds(2 * k + h, STEPS, stride=NK), :].astype(BF16)
        send_ref[k] = y[pl.ds(2 * k + 1 - h, STEPS, stride=NK), :].astype(BF16)


def partial_kernel(at_ref, og_ref, own_ref, other_ref, o_ref):
    h = at_ref[1]
    total = jnp.dot(og_ref[0, h], own_ref[...], preferred_element_type=F32)
    total += jnp.dot(og_ref[0, 1 - h], other_ref[...], preferred_element_type=F32)
    for g in range(4):
        parts = [total[q * STEPS : (q + 1) * STEPS, g * 128 : (g + 1) * 128] for q in range(4)]
        for r, out in enumerate(swap4(parts)):
            o_ref[4 * g + r, 0] = out.astype(BF16)


def backward_kernel(x_ref, prm_ref, in_ref, gy_ref, o_ref, wide, x_ext, branch, kv, rates, tails, gy, gl, long_out, states, gkv, grads, raw, small, packed):
    prepare(x_ref, prm_ref, wide, x_ext, branch)
    kv[...] = branch[1] * branch[2]
    spread(prm_ref, RATE, rates)
    decay8 = decays(prm_ref)
    weight8 = weights(prm_ref)
    for n in range(NM):
        states[n, 0:NK, :] = in_ref[n * NK : (n + 1) * NK, :]
    for v in range(2):

        def forward(t, state):
            at = pl.ds(pl.multiple_of(t * NK + v * 8, 8), 8)
            value = kv[at, :]
            state = tuple(decay8[n] * state[n] + value for n in range(NM))
            later = pl.ds(pl.multiple_of((t + 1) * NK + v * 8, 8), 8)
            for n in range(NM):
                states[n, later, :] = state[n]
            terms = [weight8[n] * state[n] for n in range(NM)]
            while len(terms) > 1:
                terms = [a + b for a, b in zip(terms[::2], terms[1::2])]
            long_out[at, :] = terms[0]
            return state

        lax.fori_loop(
            0,
            STEPS,
            forward,
            tuple(in_ref[n * NK + v * 8 : n * NK + v * 8 + 8, :] for n in range(NM)),
            unroll=2,
        )
    for k in range(NK):
        total = gy_ref[0, k % 2, k // 2].astype(F32)
        for z in range(1, 8):
            total = total + gy_ref[z, k % 2, k // 2].astype(F32)
        wide[k * STEPS : (k + 1) * STEPS, :] = total
    for t in range(STEPS):
        gy[t * NK : (t + 1) * NK, :] = wide[pl.ds(t, NK, stride=STEPS), :]
    gl[...] = gy[...] * branch[0]
    grads[0, 0:ROWS, :] = gy[...] * long_out[...]
    ends(gl, decay8, tails, True)
    tails[...] = entering(tails, rates, True)
    zero = jnp.zeros((8, 128), F32)
    for half in range(2):
        modes = range(half * 8, half * 8 + 8)
        decay = [jnp.exp(-jnp.broadcast_to(prm_ref[RATE + n : RATE + n + 1, :], (8, 128))) for n in modes]
        weight = [jnp.broadcast_to(prm_ref[RES + n : RES + n + 1, :], (8, 128)) for n in modes]
        for v in range(2):

            def backward(i, carry):
                adjoint, by_res, by_rate = carry
                t = STEPS - 1 - i
                at = pl.ds(pl.multiple_of(t * NK + v * 8, 8), 8)
                later = pl.ds(pl.multiple_of((t + 1) * NK + v * 8, 8), 8)
                value = gl[at, :]
                adjoint = tuple(decay[m] * adjoint[m] + value for m in range(8))
                by_res = tuple(by_res[m] + value * states[n, later, :] for m, n in enumerate(modes))
                by_rate = tuple(
                    by_rate[m] + adjoint[m] * states[n, at, :] for m, n in enumerate(modes)
                )
                terms = [weight[m] * adjoint[m] for m in range(8)]
                while len(terms) > 1:
                    terms = [a + b for a, b in zip(terms[::2], terms[1::2])]
                if half == 0:
                    gkv[at, :] = terms[0]
                else:
                    gkv[at, :] = gkv[at, :] + terms[0]
                return adjoint, by_res, by_rate

            zeros = tuple(zero for _ in range(8))
            first = tuple(tails[n * NK + v * 8 : n * NK + v * 8 + 8, :] for n in modes)
            _, by_res, by_rate = lax.fori_loop(0, STEPS, backward, (first, zeros, zeros), unroll=2)
            for m, n in enumerate(modes):
                rate_part = by_rate[m] * (-decay[m] * weight[m])
                to_res = pl.ds((RES + n) * 8, 8)
                to_rate = pl.ds((RATE + n) * 8, 8)
                if v == 0:
                    small[to_res, :] = by_res[m]
                    small[to_rate, :] = rate_part
                else:
                    small[to_res, :] = small[to_res, :] + by_res[m]
                    small[to_rate, :] = small[to_rate, :] + rate_part
    grads[1, 0:ROWS, :] = gkv[...] * branch[2]
    grads[2, 0:ROWS, :] = gkv[...] * branch[1]
    for p in range(3):
        for ahead in range(2):
            grads[p, ROWS + ahead * NK : ROWS + (ahead + 1) * NK, :] = shift_blocks(
                grads[p, ahead * NK : (ahead + 1) * NK, :], 1, True
            )
        total = None
        for j in range(3):
            tap = prm_ref[TAP + 3 * p + j : TAP + 3 * p + j + 1, :]
            term = tap * grads[p, j * NK : j * NK + ROWS, :]
            total = term if total is None else total + term
            product = grads[p, 0:ROWS, :] * x_ext[p, (2 - j) * NK : (2 - j) * NK + ROWS, :]
            small[pl.ds((TAP + 3 * p + j) * 8, 8), :] = jnp.sum(
                product.reshape(ROWS // 8, 8, 128), axis=0
            )
        raw[p * ROWS : (p + 1) * ROWS, :] = total
    small[pl.ds((TAP + 9) * 8, 56), :] = jnp.zeros((56, 128), F32)
    total = small[pl.ds(0, 48, stride=8), :]
    for s in range(1, 8):
        total = total + small[pl.ds(s, 48, stride=8), :]
    total = total + pltpu.roll(total, 64, 1)
    total = total + pltpu.roll(total, 32, 1)
    high = total.astype(BF16).astype(F32)
    low = total - high
    group = lane_group((24, 128))
    packed[0:24, :] = jnp.where(
        group == 0,
        high[0:24],
        jnp.where(group == 1, low[0:24], jnp.where(group == 2, high[24:48], low[24:48])),
    )
    packed[24:32, :] = jnp.zeros((8, 128), F32)
    for k in range(NK):
        for p in range(3):
            o_ref[k, p * STEPS : (p + 1) * STEPS, :] = raw[
                pl.ds(p * ROWS + k, STEPS, stride=NK), :
            ].astype(BF16)
        o_ref[k, 96:128, :] = packed[...].astype(BF16)


def unpack_kernel(x_ref, gp_ref, short_ref, res_ref, rate_ref, small):
    group = lane_group((32, 128))
    for g in range(4):
        columns = slice(g * 128, (g + 1) * 128)
        for p in range(3):
            parts = [x_ref[4 * g + r, p * STEPS : (p + 1) * STEPS, :].astype(F32) for r in range(4)]
            for q, out in enumerate(swap4(parts)):
                gp_ref[p, q * STEPS : (q + 1) * STEPS, columns] = out.astype(BF16)
        first = second = jnp.zeros((32, 128), F32)
        for r in range(4):
            pair = x_ref[4 * g + r, 96:128, :].astype(F32)
            pair = pair + pltpu.roll(pair, 96, 1)
            one = pair if r == 0 else pltpu.roll(pair, SUB * r, 1)
            two = pair if r == 2 else pltpu.roll(pair, (SUB * (r - 2)) % 128, 1)
            first = jnp.where(group == r, one, first)
            second = jnp.where(group == r, two, second)
        small[0:24, columns] = first[0:24]
        small[24:48, columns] = second[0:24]
    res_ref[...] = small[RES : RES + NM, :]
    rate_ref[...] = small[RATE : RATE + NM, :]
    for p in range(3):
        short_ref[p] = small[TAP + 3 * p : TAP + 3 * p + 3, :]


def weight_kernel(at_ref, og_ref, y_ref, own_ref, send_ref, other, y):
    h = at_ref[1]
    step = pl.program_id(0)
    for g in range(4):
        parts = [y_ref[2 * g + r // 2, jnp.bitwise_xor(r % 2, h), 0].astype(F32) for r in range(4)]
        for q, out in enumerate(swap4(parts)):
            y[q * STEPS : (q + 1) * STEPS, g * 128 : (g + 1) * 128] = out.astype(BF16)
    over_rows = (((0,), (0,)), ((), ()))
    mine = lax.dot_general(og_ref[0, h], y[...], over_rows, preferred_element_type=F32)
    theirs = lax.dot_general(og_ref[0, 1 - h], y[...], over_rows, preferred_element_type=F32)

    @pl.when(step == 0)
    def _():
        own_ref[...] = mine
        other[...] = theirs

    @pl.when(step > 0)
    def _():
        own_ref[...] += mine
        other[...] += theirs

    @pl.when(step == pl.num_programs(0) - 1)
    def _():
        send_ref[...] = other[...].astype(BF16)


def shape(dims, dtype=F32):
    return jax.ShapeDtypeStruct(dims, dtype)


def scratch(*dims):
    return pltpu.VMEM(dims, F32)


SCANS = [
    scratch(NK * 96, 128),
    scratch(3, ROWS + 2 * NK, 128),
    scratch(3, ROWS, 128),
    scratch(ROWS, 128),
    scratch(NM * NK, 128),
    scratch(NM * NK, 128),
]
SWAP = [(0, 1), (1, 0)]


def on_device(out_grad, out_weight, projections, short_filters, residues, decay_rates):
    z, h = lax.axis_index("z"), lax.axis_index("xh")
    here = jnp.stack([z, h]).astype(jnp.int32)

    planes, spots = [], []
    for zz in range(8):
        for xl in range(2):
            for yy in range(4):
                to = 4 * xl + yy
                spot = (to - zz) % 8
                at = zz * 8 + xl * 4 + yy
                planes.append((at, zz * 8 + spot))
                spots.append((zz * 8 + spot, to * 8 + spot))
    moved = lax.ppermute(out_grad, ("z", "xl", "y"), planes)
    moved = lax.ppermute(moved, ("z", "xl", "y"), spots)
    other_weight = lax.ppermute(out_weight, "xh", SWAP)
    og = lax.all_gather(moved, FSDP, axis=0).reshape(8, 2, 128, 512)

    chunks = pl.pallas_call(pack_kernel, out_shape=shape((NK, 96, 128), BF16), in_specs=[VMEM], out_specs=VMEM)(projections)
    x = lax.all_to_all(chunks, CTX, 0, 0)
    prm = jnp.concatenate([residues, decay_rates, short_filters.reshape(9, 512)], axis=0)
    prm = lax.dynamic_slice(prm, (0, (2 * z + h) * SUB), (41, SUB))
    prm = jnp.pad(jnp.tile(prm, (1, 4)), ((0, 7), (0, 0)))

    keep, send, state_in = pl.pallas_call(
        forward_kernel,
        out_shape=(shape((8, STEPS, 128), BF16), shape((8, STEPS, 128), BF16), shape((NM * NK, 128))),
        in_specs=[pl.BlockSpec(memory_space=pltpu.SMEM), VMEM, VMEM],
        out_specs=(VMEM, VMEM, VMEM),
        scratch_shapes=SCANS + [scratch(ROWS, 128)],
        compiler_params=PARAMS,
    )(here[1:], x, prm)
    y = lax.all_gather(jnp.stack([keep, lax.ppermute(send, "xh", SWAP)]), "z", axis=0)

    parts = pl.pallas_call(
        partial_kernel,
        out_shape=shape((NK, 8, STEPS, 128), BF16),
        grid_spec=pltpu.PrefetchScalarGridSpec(
            num_scalar_prefetch=1,
            grid=(8,),
            in_specs=[
                pl.BlockSpec((1, 2, 128, 512), lambda p, at: (p, 0, 0, 0)),
                pl.BlockSpec((512, 512), lambda p, at: (0, 0)),
                pl.BlockSpec((512, 512), lambda p, at: (0, 0)),
            ],
            out_specs=pl.BlockSpec((NK, 1, STEPS, 128), lambda p, at: (0, (at[0] - p + 8) % 8, 0, 0)),
        ),
        compiler_params=PARAMS,
    )(here, og, out_weight, other_weight)
    grad_y = lax.all_to_all(parts, CTX, 0, 0).reshape(8, 2, 8, STEPS, 128)

    out = pl.pallas_call(
        backward_kernel,
        out_shape=shape((NK, 128, 128), BF16),
        in_specs=[VMEM] * 4,
        out_specs=VMEM,
        scratch_shapes=SCANS
        + [scratch(ROWS, 128)] * 3
        + [scratch(NM, ROWS + NK, 128), scratch(ROWS, 128), scratch(3, ROWS + 2 * NK, 128)]
        + [scratch(3 * ROWS, 128), scratch(48 * 8, 128), scratch(32, 128)],
        compiler_params=PARAMS,
    )(x, prm, state_in, grad_y)
    back = lax.all_to_all(out, CTX, 0, 0)
    grad_projections, grad_short, grad_res, grad_rate = pl.pallas_call(
        unpack_kernel,
        out_shape=(shape((3, 128, 512), BF16), shape((3, 3, 512)), shape((NM, 512)), shape((NM, 512))),
        in_specs=[VMEM],
        out_specs=(VMEM,) * 4,
        scratch_shapes=[scratch(48, 512)],
    )(back)

    own, send = pl.pallas_call(
        weight_kernel,
        out_shape=(shape((512, 512)), shape((512, 512), BF16)),
        grid_spec=pltpu.PrefetchScalarGridSpec(
            num_scalar_prefetch=1,
            grid=(8,),
            in_specs=[
                pl.BlockSpec((1, 2, 128, 512), lambda p, at: (p, 0, 0, 0)),
                pl.BlockSpec((8, 2, 1, STEPS, 128), lambda p, at: (0, 0, (at[0] - p + 8) % 8, 0, 0)),
            ],
            out_specs=[pl.BlockSpec((512, 512), lambda p, at: (0, 0))] * 2,
            scratch_shapes=[scratch(512, 512), pltpu.VMEM((128, 512), BF16)],
        ),
        compiler_params=PARAMS,
    )(here, og, y)
    grad_weight = (own + lax.ppermute(send, "xh", SWAP).astype(F32)).astype(BF16)
    return grad_weight, grad_projections, grad_short, grad_res, grad_rate


def solution(mesh):
    fine = Mesh(mesh.devices.reshape(8, 2, 2, 4, 2), CTX + FSDP)
    placed = (
        P(CTX, FSDP),
        P(CTX, FSDP),
        P(None, CTX, FSDP),
        P(None, None, FSDP),
        P(None, FSDP),
        P(None, FSDP),
    )
    return jax.shard_map(
        on_device,
        mesh=fine,
        in_specs=placed,
        out_specs=(
            P(CTX, FSDP),
            P(None, CTX, FSDP),
            P(None, None, FSDP),
            P(None, FSDP),
            P(None, FSDP),
        ),
        check_vma=False,
    )
```

time: 874 us -> 186 us (0.21)
  waiting for transfers between devices: 559 us -> 85.3 us
  blocking collectives: 126 us -> 0 us
  other arithmetic: 127 us -> 1.78 us
  starting transfers between devices: 6.51 us -> 45 us
  Pallas kernels: 0 us -> 25.6 us
  matrix products: 13.4 us -> 0 us
  local copies, waits for them, and re-layouts: 21.9 us -> 12.2 us
    reduce_scatter x1 -> x0, waiting for transfers between devices: 289 us -> none  [on_device(): lax.psum_scatter(lax.dot_general(columns, y_rounded, (((0,), (0,)), ((),...]
    psum x1 -> x0, waiting for transfers between devices: 149 us -> none  [on_device(): lax.psum((filter_part, grad_res_part, grad_rate_part), 'ctx')]
    all_gather x3 -> x0, blocking collectives: 126 us -> none  [carried_in(): everything = jax.tree.map(lambda part: lax.all_gather(part, axis), array)]
    all_gather x2, waiting for transfers between devices: 114 us -> 33.8 us  [the longest x1 19.5 us: on_device(): lax.all_gather(jnp.stack([keep, lax.ppermute(send, 'xh', SWAP)]), 'z', ax...]
    unnamed x62 -> x0, other arithmetic: 68.5 us -> none
    ppermute x2 -> x5, waiting for transfers between devices: 5.16 us -> 34.3 us  [the longest x1 14.9 us: on_device(): other_weight = lax.ppermute(out_weight, 'xh', SWAP)]
    pallas_call x0 -> x6, Pallas kernels: none -> 25.6 us  [the longest x1 7.53 us: on_device(): pl.pallas_call(weight_kernel, out_shape=(shape((512, 512)), shape((512, 5...]
    select_n x32 -> x0, other arithmetic: 24.7 us -> none  [lap(): return jax.tree.map(lambda a, b: jnp.where(reached, a, b), new, before)]
  transfers between devices with their start and end apart: 6 -> 10, of which waited for: 4 -> 7; matrix products, arithmetic and copies ran while one was open for 3% -> 3% of each run, Pallas kernels for 0% -> 12%
where the time goes in v1:
time: 186 us; the launch traced here: 185 us
  waiting for transfers between devices  85.3 us (46%)
  starting transfers between devices  45 us (24%)
  Pallas kernels  25.6 us (14%)
  between operations  15.6 us (8%)
  local copies, waits for them, and re-layouts  12.2 us (7%)
    all_gather x1, waiting for transfers between devices, on_device(): lax.all_gather(jnp.stack([keep, lax.ppermute(send, 'xh', SWAP)]), 'z', ax...  19.5 us
    all_to_all x1, waiting for transfers between devices, on_device(): grad_y = lax.all_to_all(parts, CTX, 0, 0).reshape(8, 2, 8, STEPS, 128)  17.2 us
    ppermute x1, waiting for transfers between devices, on_device(): other_weight = lax.ppermute(out_weight, 'xh', SWAP)  14.9 us
    all_gather x1, waiting for transfers between devices, on_device(): og = lax.all_gather(moved, FSDP, axis=0).reshape(8, 2, 128, 512)  14.2 us
    ppermute x1, starting transfers between devices, on_device(): moved = lax.ppermute(moved, ('z', 'xl', 'y'), spots)  13.3 us
    ppermute x1, waiting for transfers between devices, on_device(): lax.ppermute(send, 'xh', SWAP).astype(F32)  9.35 us
    unnamed x28, local copies, waits for them, and re-layouts  9.01 us
    all_to_all x1, starting transfers between devices, on_device(): grad_y = lax.all_to_all(parts, CTX, 0, 0).reshape(8, 2, 8, STEPS, 128)  8.93 us
  transfers between devices with their start and end apart: 10, of which 7 were waited for; matrix products, arithmetic and copies ran while one was open for 3% of the time, Pallas kernels for 12%

profile of v1, /device:TPU:16, one launch (start us, length us, event | category | flops | bytes accessed | tf_op | source)
XLA Modules:
  0.0 185.5 jit_solution(1832676845486158637)
XLA Ops:
  8.0 1.6 collective-permute-start
  9.6 13.3 %collective-permute-start.1 = (bf16[128,512]{1,0:T(8,128)(2,1)S(1)}, bf16[128,512]{1,0:T(8,128)(2,1)S(1)}, u32[]{:S(2)}, u32[]{:S(2)}) collective-permute-start(bf16[128,512]{1,0:T(8,128)(2,1)S(1)} %collective-permute-done), channel_id=1, source_target_pairs={{0,0},{2,34},{4,68},{6,102},{8,136},{10,170},{12,204},{14,238},{46... | collective-permute-start | bytes 393224 | tf_op jit(solution)/shard_map/ppermute | solution.py:375
  23.0 7.6 %collective-permute-done.1 = bf16[128,512]{1,0:T(8,128)(2,1)S(1)} collective-permute-done((bf16[128,512]{1,0:T(8,128)(2,1)S(1)}, bf16[128,512]{1,0:T(8,128)(2,1)S(1)}, u32[]{:S(2)}, u32[]{:S(2)}) %collective-permute-start.1) | collective-permute-done | bytes 131104 | tf_op jit(solution)/shard_map/ppermute | solution.py:375
  31.2 2.1 %shard_map.101 = bf16[16,96,128]{2,1,0:T(8,128)(2,1)} custom-call(bf16[3,128,512]{2,1,0:T(8,128)(2,1)} %x_ref.1), custom_call_target="tpu_custom_call" | custom-call | tf_op jit(solution)/shard_map/pallas_call | solution.py:379
  33.3 7.5 %all-to-all-start = ((bf16[16,96,128]{2,1,0:T(8,128)(2,1)}), bf16[16,96,128]{2,1,0:T(8,128)(2,1)S(1)}, u32[]{:S(2)}, u32[]{:S(2)}) async-start(bf16[16,96,128]{2,1,0:T(8,128)(2,1)} %shard_map.101), calls=%async_computation | async-start | bytes 786432 | tf_op jit(solution)/shard_map/all_to_all | solution.py:380
  40.8 3.4 %collective-permute-start.4 = (bf16[512,512]{1,0:T(8,128)(2,1)}, bf16[512,512]{1,0:T(8,128)(2,1)S(1)}, u32[]{:S(2)}, u32[]{:S(2)}) collective-permute-start(bf16[512,512]{1,0:T(8,128)(2,1)} %own_ref.1), channel_id=1, source_target_pairs={{0,16},{16,0},{1,17},{17,1},{2,18},{18,2},{3,19},{19,3},{4,20},{20... | collective-permute-start | bytes 1572872 | tf_op jit(solution)/shard_map/ppermute | solution.py:376
  44.3 14.9 %collective-permute-done.4.other_ref = bf16[512,512]{1,0:T(8,128)(2,1)S(1)} collective-permute-done((bf16[512,512]{1,0:T(8,128)(2,1)}, bf16[512,512]{1,0:T(8,128)(2,1)S(1)}, u32[]{:S(2)}, u32[]{:S(2)}) %collective-permute-start.4) | collective-permute-done | bytes 524320 | tf_op jit(solution)/shard_map/ppermute | solution.py:376
  59.3 14.2 %all-gather.5.cloned.1.call-done = bf16[2048,512]{1,0:T(8,128)(2,1)} async-done(((bf16[128,512]{1,0:T(8,128)(2,1)}), bf16[2048,512]{1,0:T(8,128)(2,1)}) %all-gather.5.cloned.1.call-update) | async-done | bytes 2097168 | tf_op jit(solution)/shard_map/all_gather | solution.py:377
  73.5 1.6 copy-done
  76.1 5.5 %shard_map.104 = bf16[16,8,32,128]{3,2,1,0:T(8,128)(2,1)} custom-call(s32[2]{0:T(128)S(1)} %pad_add_fusion.at_ref, bf16[8,2,128,512]{3,2,1,0:T(8,128)(2,1)S(1)} %bitcast.7, bf16[512,512]{1,0:T(8,128)(2,1)S(1)} %copy-done.4, bf16[512,512]{1,0:T(8,128)(2,1)S(1)} %collective-permute-done.4.other_ref), custom_call_target="tpu_custom_call" | custom-call | tf_op jit(solution)/shard_map/pallas_call | solution.py:395
  81.7 8.9 %all-to-all-start.1 = ((bf16[16,8,32,128]{3,2,1,0:T(8,128)(2,1)}), bf16[16,8,32,128]{3,2,1,0:T(8,128)(2,1)S(1)}, u32[]{:S(2)}, u32[]{:S(2)}) async-start(bf16[16,8,32,128]{3,2,1,0:T(8,128)(2,1)} %shard_map.104), calls=%async_computation.1 | async-start | bytes 2097152 | tf_op jit(solution)/shard_map/all_to_all | solution.py:410
  91.4 1.7 tile.10
  93.9 2.3 %shard_map.102 = (bf16[8,32,128]{2,1,0:T(8,128)(2,1)S(1)}, bf16[8,32,128]{2,1,0:T(8,128)(2,1)S(1)}, f32[256,128]{1,0:T(8,128)S(1)}) custom-call(s32[1]{0:T(128)} %bitcast.1.h_ref, bf16[16,96,128]{2,1,0:T(8,128)(2,1)S(1)} %all-to-all-done.x_ref, f32[48,128]{1,0:T(8,128)S(1)} %pad.4.prm_ref), custom_call_target="tpu_custom_call" | custom-call | tf_op jit(solution)/shard_map/pallas_call | solution.py:385
  97.5 3.4 %collective-permute-start.2 = (bf16[8,32,128]{2,1,0:T(8,128)(2,1)S(1)}, bf16[8,32,128]{2,1,0:T(8,128)(2,1)S(1)}, u32[]{:S(2)}, u32[]{:S(2)}) collective-permute-start(bf16[8,32,128]{2,1,0:T(8,128)(2,1)S(1)} %get-tuple-element.15), channel_id=1, source_target_pairs={{0,16},{16,0},{1,17},{17,1},{2,18},{18,2},{3,19},{19,3},{4,20},{20... | collective-permute-start | bytes 196616 | tf_op jit(solution)/shard_map/ppermute | solution.py:393
  100.9 2.5 %collective-permute-done.2 = bf16[8,32,128]{2,1,0:T(8,128)(2,1)S(1)} collective-permute-done((bf16[8,32,128]{2,1,0:T(8,128)(2,1)S(1)}, bf16[8,32,128]{2,1,0:T(8,128)(2,1)S(1)}, u32[]{:S(2)}, u32[]{:S(2)}) %collective-permute-start.2) | collective-permute-done | bytes 65568 | tf_op jit(solution)/shard_map/ppermute | solution.py:393
  104.0 17.2 %all-to-all-done.1 = bf16[16,8,32,128]{3,2,1,0:T(8,128)(2,1)S(1)} async-done(((bf16[16,8,32,128]{3,2,1,0:T(8,128)(2,1)}), bf16[16,8,32,128]{3,2,1,0:T(8,128)(2,1)S(1)}, u32[]{:S(2)}, u32[]{:S(2)}) %all-to-all-start.1) | async-done | bytes 1048608 | tf_op jit(solution)/shard_map/all_to_all | solution.py:410
  122.9 5.1 %shard_map.105 = bf16[16,128,128]{2,1,0:T(8,128)(2,1)S(1)} custom-call(bf16[16,96,128]{2,1,0:T(8,128)(2,1)S(1)} %all-to-all-done.x_ref, f32[48,128]{1,0:T(8,128)S(1)} %copy-done.6, f32[256,128]{1,0:T(8,128)S(1)} %copy-done.8, bf16[8,2,8,32,128]{4,3,2,1,0:T(8,128)(2,1)S(1)} %bitcast.9), custom_call_target="tpu_custom_call" | custom-call | tf_op jit(solution)/shard_map/pallas_call | solution.py:412
  128.7 3.6 %all-to-all-start.2 = ((bf16[16,128,128]{2,1,0:T(8,128)(2,1)}), bf16[16,128,128]{2,1,0:T(8,128)(2,1)S(1)}, u32[]{:S(2)}, u32[]{:S(2)}) async-start(bf16[16,128,128]{2,1,0:T(8,128)(2,1)} %copy-done.2), calls=%async_computation.2 | async-start | bytes 1048576 | tf_op jit(solution)/shard_map/all_to_all | solution.py:423
  132.3 19.5 %all-gather.7.cloned.1.call-done = bf16[16,8,32,128]{3,2,1,0:T(8,128)(2,1)} async-done(((bf16[2,8,32,128]{3,2,1,0:T(8,128)(2,1)}), bf16[16,8,32,128]{3,2,1,0:T(8,128)(2,1)}) %all-gather.7.cloned.1.call-update) | async-done | bytes 1048592 | tf_op jit(solution)/shard_map/all_gather | solution.py:393
  151.9 1.2 copy-done.3
  153.1 7.5 %shard_map.103 = (f32[512,512]{1,0:T(8,128)S(1)}, bf16[512,512]{1,0:T(8,128)(2,1)S(1)}) custom-call(s32[2]{0:T(128)S(1)} %pad_add_fusion.at_ref, bf16[8,2,128,512]{3,2,1,0:T(8,128)(2,1)S(1)} %bitcast.8, bf16[8,2,8,32,128]{4,3,2,1,0:T(8,128)(2,1)S(1)} %bitcast.10), custom_call_target="tpu_custom_call" | custom-call | tf_op jit(solution)/shard_map/pallas_call | solution.py:432
  160.6 3.2 %collective-permute-start.3 = (bf16[512,512]{1,0:T(8,128)(2,1)S(1)}, bf16[512,512]{1,0:T(8,128)(2,1)S(1)}, u32[]{:S(2)}, u32[]{:S(2)}) collective-permute-start(bf16[512,512]{1,0:T(8,128)(2,1)S(1)} %get-tuple-element.17), channel_id=1, source_target_pairs={{0,16},{16,0},{1,17},{17,1},{2,18},{18,2},{3,19},{19,3},{4,20},{20... | collective-permute-start | bytes 1572872 | tf_op jit(solution)/shard_map/ppermute | solution.py:447
  163.8 9.3 %collective-permute-done.3 = bf16[512,512]{1,0:T(8,128)(2,1)S(1)} collective-permute-done((bf16[512,512]{1,0:T(8,128)(2,1)S(1)}, bf16[512,512]{1,0:T(8,128)(2,1)S(1)}, u32[]{:S(2)}, u32[]{:S(2)}) %collective-permute-start.3) | collective-permute-done | bytes 524320 | tf_op jit(solution)/shard_map/ppermute | solution.py:447
  174.9 3.1 %shard_map.106 = (bf16[3,128,512]{2,1,0:T(8,128)(2,1)}, f32[3,3,512]{2,1,0:T(4,128)}, f32[16,512]{1,0:T(8,128)}, f32[16,512]{1,0:T(8,128)}) custom-call(bf16[16,128,128]{2,1,0:T(8,128)(2,1)} %copy-done.9), custom_call_target="tpu_custom_call" | custom-call | tf_op jit(solution)/shard_map/pallas_call | solution.py:424
  (40 shorter events, 9.5 us)
Async XLA Ops:
  8.0 65.5 %all-gather.5.cloned.1.call-start = ((), (), s32[]{:S(2)}) async-start(), calls=%async_computation.3 | async-start | bytes 2228224 | tf_op jit(solution)/shard_map/all_gather | solution.py:377
  8.0 1.6 collective-permute-start
  9.6 20.9 %collective-permute-start.1 = (bf16[128,512]{1,0:T(8,128)(2,1)S(1)}, bf16[128,512]{1,0:T(8,128)(2,1)S(1)}, u32[]{:S(2)}, u32[]{:S(2)}) collective-permute-start(bf16[128,512]{1,0:T(8,128)(2,1)S(1)} %collective-permute-done), channel_id=1, source_target_pairs={{0,0},{2,34},{4,68},{6,102},{8,136},{10,170},{12,204},{14,238},{46... | collective-permute-start | bytes 393224 | tf_op jit(solution)/shard_map/ppermute | solution.py:375
  30.5 0.7 copy-start.10
  33.3 48.3 %all-to-all-start = ((bf16[16,96,128]{2,1,0:T(8,128)(2,1)}), bf16[16,96,128]{2,1,0:T(8,128)(2,1)S(1)}, u32[]{:S(2)}, u32[]{:S(2)}) async-start(bf16[16,96,128]{2,1,0:T(8,128)(2,1)} %shard_map.101), calls=%async_computation | async-start | bytes 786432 | tf_op jit(solution)/shard_map/all_to_all | solution.py:380
  40.8 18.5 %collective-permute-start.4 = (bf16[512,512]{1,0:T(8,128)(2,1)}, bf16[512,512]{1,0:T(8,128)(2,1)S(1)}, u32[]{:S(2)}, u32[]{:S(2)}) collective-permute-start(bf16[512,512]{1,0:T(8,128)(2,1)} %own_ref.1), channel_id=1, source_target_pairs={{0,16},{16,0},{1,17},{17,1},{2,18},{18,2},{3,19},{19,3},{4,20},{20... | collective-permute-start | bytes 1572872 | tf_op jit(solution)/shard_map/ppermute | solution.py:376
  73.5 1.6 copy-start
  75.1 1.0 copy-start.4
  81.7 9.0 %copy-start.13 = (f32[3,3,512]{2,1,0:T(4,128)S(1)}, f32[3,3,512]{2,1,0:T(4,128)}, u32[]{:S(2)}) copy-start(f32[3,3,512]{2,1,0:T(4,128)} %param.9) | copy-start | bytes 55300
  81.7 9.0 %copy-start.11 = (f32[16,512]{1,0:T(8,128)S(1)}, f32[16,512]{1,0:T(8,128)}, u32[]{:S(2)}) copy-start(f32[16,512]{1,0:T(8,128)} %param.10) | copy-start | bytes 98308
  81.7 9.0 %copy-start.12 = (f32[16,512]{1,0:T(8,128)S(1)}, f32[16,512]{1,0:T(8,128)}, u32[]{:S(2)}) copy-start(f32[16,512]{1,0:T(8,128)} %param.11) | copy-start | bytes 98308
  81.7 39.6 %all-to-all-start.1 = ((bf16[16,8,32,128]{3,2,1,0:T(8,128)(2,1)}), bf16[16,8,32,128]{3,2,1,0:T(8,128)(2,1)S(1)}, u32[]{:S(2)}, u32[]{:S(2)}) async-start(bf16[16,8,32,128]{3,2,1,0:T(8,128)(2,1)} %shard_map.104), calls=%async_computation.1 | async-start | bytes 2097152 | tf_op jit(solution)/shard_map/all_to_all | solution.py:410
  90.6 61.3 %all-gather.7.cloned.1.call-start = ((), (), s32[]{:S(2)}) async-start(), calls=%async_computation.4 | async-start | bytes 1179648 | tf_op jit(solution)/shard_map/all_gather | solution.py:393
  91.4 60.4 %copy-start.1 = (bf16[2048,512]{1,0:T(8,128)(2,1)S(1)}, bf16[2048,512]{1,0:T(8,128)(2,1)}, u32[]{:S(2)}) copy-start(bf16[2048,512]{1,0:T(8,128)(2,1)} %all-gather.5.cloned.1.call-done) | copy-start | bytes 6291460
  96.2 0.6 copy-start.5
  96.8 0.7 copy-start.7
  97.5 5.9 %collective-permute-start.2 = (bf16[8,32,128]{2,1,0:T(8,128)(2,1)S(1)}, bf16[8,32,128]{2,1,0:T(8,128)(2,1)S(1)}, u32[]{:S(2)}, u32[]{:S(2)}) collective-permute-start(bf16[8,32,128]{2,1,0:T(8,128)(2,1)S(1)} %get-tuple-element.15), channel_id=1, source_target_pairs={{0,16},{16,0},{1,17},{17,1},{2,18},{18,2},{3,19},{19,3},{4,20},{20... | collective-permute-start | bytes 196616 | tf_op jit(solution)/shard_map/ppermute | solution.py:393
  121.2 0.7 copy-start.6
  122.0 0.9 copy-start.8
  127.9 0.8 copy-start.2
  128.7 45.4 %all-to-all-start.2 = ((bf16[16,128,128]{2,1,0:T(8,128)(2,1)}), bf16[16,128,128]{2,1,0:T(8,128)(2,1)S(1)}, u32[]{:S(2)}, u32[]{:S(2)}) async-start(bf16[16,128,128]{2,1,0:T(8,128)(2,1)} %copy-done.2), calls=%async_computation.2 | async-start | bytes 1048576 | tf_op jit(solution)/shard_map/all_to_all | solution.py:423
  151.9 1.2 copy-start.3
  160.6 12.5 %collective-permute-start.3 = (bf16[512,512]{1,0:T(8,128)(2,1)S(1)}, bf16[512,512]{1,0:T(8,128)(2,1)S(1)}, u32[]{:S(2)}, u32[]{:S(2)}) collective-permute-start(bf16[512,512]{1,0:T(8,128)(2,1)S(1)} %get-tuple-element.17), channel_id=1, source_target_pairs={{0,16},{16,0},{1,17},{17,1},{2,18},{18,2},{3,19},{19,3},{4,20},{20... | collective-permute-start | bytes 1572872 | tf_op jit(solution)/shard_map/ppermute | solution.py:447
  174.1 0.8 copy-start.9
Sparse Core Ops, SparseCore 0:
  31.3 42.1 all-gather.4
Sparse Core Ops, SparseCore 1:
  104.1 47.7 all-gather.6

commit v2 on v1

--- a/solution.py
+++ b/solution.py
@@ -5,6 +5,7 @@
 from jax.experimental.pallas import tpu as pltpu
 from jax.sharding import Mesh
 from jax.sharding import PartitionSpec as P
+
 
 F32 = jnp.float32
 BF16 = jnp.bfloat16
@@ -55,7 +56,7 @@
     return jnp.where(group < blocks, over, turned)
 
 
-def pack_kernel(x_ref, o_ref):
+def pack_kernel(at_ref, x_ref, res_ref, rate_ref, tap_ref, o_ref, prm_ref):
     for p in range(3):
         for g in range(4):
             parts = [
@@ -64,6 +65,19 @@
             ]
             for r, out in enumerate(swap4(parts)):
                 o_ref[4 * g + r, p * STEPS : (p + 1) * STEPS, :] = out.astype(BF16)
+    m = at_ref[0]
+    columns = pl.ds(pl.multiple_of(m // 4 * 128, 128), 128)
+
+    def own(values):
+        values = pltpu.roll(values, (4 - m % 4) % 4 * SUB, 1)
+        values = jnp.where(lane_group(values.shape) == 0, values, 0.0)
+        values = values + pltpu.roll(values, 64, 1)
+        return values + pltpu.roll(values, 32, 1)
+
+    prm_ref[RES : RES + NM, :] = own(res_ref[:, columns])
+    prm_ref[RATE : RATE + NM, :] = own(rate_ref[:, columns])
+    for p in range(3):
+        prm_ref[TAP + 8 * p : TAP + 8 * p + 3, :] = own(tap_ref[p, :, columns])
 
 
 def prepare(x_ref, prm_ref, wide, x_ext, branch):
@@ -77,7 +91,7 @@
             )
         total = None
         for j in range(3):
-            tap = prm_ref[TAP + 3 * p + j : TAP + 3 * p + j + 1, :]
+            tap = prm_ref[TAP + 8 * p + j : TAP + 8 * p + j + 1, :]
             term = tap * x_ext[p, (2 - j) * NK : (2 - j) * NK + ROWS, :]
             total = term if total is None else total + term
         branch[p] = total
@@ -125,7 +139,7 @@
     return [jnp.broadcast_to(prm_ref[RES + n : RES + n + 1, :], (8, 128)) for n in range(NM)]
 
 
-def forward_kernel(h_ref, x_ref, prm_ref, keep_ref, send_ref, in_ref, wide, x_ext, branch, kv, rates, tails, y):
+def forward_kernel(at_ref, x_ref, prm_ref, keep_ref, send_ref, in_ref, wide, x_ext, branch, kv, rates, tails, y):
     prepare(x_ref, prm_ref, wide, x_ext, branch)
     kv[...] = branch[1] * branch[2]
     spread(prm_ref, RATE, rates)
@@ -152,23 +166,38 @@
             tuple(in_ref[n * NK + v * 8 : n * NK + v * 8 + 8, :] for n in range(NM)),
             unroll=2,
         )
-    h = h_ref[0]
+    h = at_ref[1]
     for k in range(8):
         keep_ref[k] = y[pl.ds(2 * k + h, STEPS, stride=NK), :].astype(BF16)
         send_ref[k] = y[pl.ds(2 * k + 1 - h, STEPS, stride=NK), :].astype(BF16)
 
 
-def partial_kernel(at_ref, og_ref, own_ref, other_ref, o_ref):
-    h = at_ref[1]
-    total = jnp.dot(og_ref[0, h], own_ref[...], preferred_element_type=F32)
-    total += jnp.dot(og_ref[0, 1 - h], other_ref[...], preferred_element_type=F32)
-    for g in range(4):
-        parts = [total[q * STEPS : (q + 1) * STEPS, g * 128 : (g + 1) * 128] for q in range(4)]
-        for r, out in enumerate(swap4(parts)):
-            o_ref[4 * g + r, 0] = out.astype(BF16)
-
-
-def backward_kernel(x_ref, prm_ref, in_ref, gy_ref, o_ref, wide, x_ext, branch, kv, rates, tails, gy, gl, long_out, states, gkv, grads, raw, small, packed):
+BATCHES = ((0, 4, 1, 3), (5, 7, 2, 6))
+
+
+def shard_of(z, spot, away):
+    return (z - jnp.bitwise_xor(spot, away) + 8) % 8
+
+
+def partial_kernel(at_ref, mine_ref, theirs_ref, w0_ref, w1_ref, after_ref, o_ref, rows_ref):
+    own_first = at_ref[1] == at_ref[2]
+    for i in range(4):
+        mine, theirs = mine_ref[i], theirs_ref[i]
+        rows_ref[0, i * 128 : (i + 1) * 128, :] = jnp.where(own_first, mine, theirs)
+        rows_ref[1, i * 128 : (i + 1) * 128, :] = jnp.where(own_first, theirs, mine)
+    for i in range(4):
+        total = jnp.dot(
+            rows_ref[0, i * 128 : (i + 1) * 128, :], w0_ref[...], preferred_element_type=F32
+        ) + jnp.dot(
+            rows_ref[1, i * 128 : (i + 1) * 128, :], w1_ref[...], preferred_element_type=F32
+        )
+        for g in range(4):
+            parts = [total[q * STEPS : (q + 1) * STEPS, g * 128 : (g + 1) * 128] for q in range(4)]
+            for r, out in enumerate(swap4(parts)):
+                o_ref[4 * g + r, i] = out.astype(BF16)
+
+
+def backward_kernel(at_ref, x_ref, prm_ref, in_ref, gy1_ref, gy2_ref, o_ref, wide, x_ext, branch, kv, rates, tails, gy, gl, long_out, states, gkv, grads, raw, small, packed):
     prepare(x_ref, prm_ref, wide, x_ext, branch)
     kv[...] = branch[1] * branch[2]
     spread(prm_ref, RATE, rates)
@@ -198,11 +227,14 @@
             tuple(in_ref[n * NK + v * 8 : n * NK + v * 8 + 8, :] for n in range(NM)),
             unroll=2,
         )
-    for k in range(NK):
-        total = gy_ref[0, k % 2, k // 2].astype(F32)
-        for z in range(1, 8):
-            total = total + gy_ref[z, k % 2, k // 2].astype(F32)
-        wide[k * STEPS : (k + 1) * STEPS, :] = total
+    spot = at_ref[3]
+    wide[0:ROWS, :] = jnp.zeros((ROWS, 128), F32)
+    for batch, gy_ref in zip(BATCHES, (gy1_ref, gy2_ref)):
+        for i, away in enumerate(batch):
+            for source in range(NK):
+                k = 2 * shard_of(source // 2, spot, away) + source % 2
+                at = pl.ds(pl.multiple_of(k * STEPS, STEPS), STEPS)
+                wide[at, :] = wide[at, :] + gy_ref[source, i].astype(F32)
     for t in range(STEPS):
         gy[t * NK : (t + 1) * NK, :] = wide[pl.ds(t, NK, stride=STEPS), :]
     gl[...] = gy[...] * branch[0]
@@ -258,7 +290,7 @@
             )
         total = None
         for j in range(3):
-            tap = prm_ref[TAP + 3 * p + j : TAP + 3 * p + j + 1, :]
+            tap = prm_ref[TAP + 8 * p + j : TAP + 8 * p + j + 1, :]
             term = tap * grads[p, j * NK : j * NK + ROWS, :]
             total = term if total is None else total + term
             product = grads[p, 0:ROWS, :] * x_ext[p, (2 - j) * NK : (2 - j) * NK + ROWS, :]
@@ -313,30 +345,28 @@
         short_ref[p] = small[TAP + 3 * p : TAP + 3 * p + 3, :]
 
 
-def weight_kernel(at_ref, og_ref, y_ref, own_ref, send_ref, other, y):
-    h = at_ref[1]
-    step = pl.program_id(0)
-    for g in range(4):
-        parts = [y_ref[2 * g + r // 2, jnp.bitwise_xor(r % 2, h), 0].astype(F32) for r in range(4)]
-        for q, out in enumerate(swap4(parts)):
-            y[q * STEPS : (q + 1) * STEPS, g * 128 : (g + 1) * 128] = out.astype(BF16)
+def weight_kernel(at_ref, rows1_ref, rows2_ref, y0, r1, r2, r3, r4, l3, l2, l1, own_ref, send_ref, y_all, y):
+    z, h, spot = at_ref[0], at_ref[1], at_ref[3]
+    for back, y_ref in enumerate((y0, r1, r2, r3, r4, l3, l2, l1)):
+        y_all[(z - back + 8) % 8] = y_ref[...]
+    for b, batch in enumerate(BATCHES):
+        for i, away in enumerate(batch):
+            k = shard_of(z, spot, away)
+            for g in range(4):
+                parts = [
+                    y_all[2 * g + r // 2, jnp.bitwise_xor(r % 2, h), k].astype(F32)
+                    for r in range(4)
+                ]
+                for q, out in enumerate(swap4(parts)):
+                    first = b * 512 + i * 128 + q * STEPS
+                    y[first : first + STEPS, g * 128 : (g + 1) * 128] = out.astype(BF16)
     over_rows = (((0,), (0,)), ((), ()))
-    mine = lax.dot_general(og_ref[0, h], y[...], over_rows, preferred_element_type=F32)
-    theirs = lax.dot_general(og_ref[0, 1 - h], y[...], over_rows, preferred_element_type=F32)
-
-    @pl.when(step == 0)
-    def _():
-        own_ref[...] = mine
-        other[...] = theirs
-
-    @pl.when(step > 0)
-    def _():
-        own_ref[...] += mine
-        other[...] += theirs
-
-    @pl.when(step == pl.num_programs(0) - 1)
-    def _():
-        send_ref[...] = other[...].astype(BF16)
+    for x, out_ref in enumerate((own_ref, send_ref)):
+        total = lax.dot_general(rows1_ref[x], y[0:512, :], over_rows, preferred_element_type=F32)
+        total += lax.dot_general(
+            rows2_ref[x], y[512:1024, :], over_rows, preferred_element_type=F32
+        )
+        out_ref[...] = total.astype(out_ref.dtype)
 
 
 def shape(dims, dtype=F32):
@@ -355,73 +385,88 @@
     scratch(NM * NK, 128),
     scratch(NM * NK, 128),
 ]
-SWAP = [(0, 1), (1, 0)]
-
-
-def on_device(out_grad, out_weight, projections, short_filters, residues, decay_rates):
-    z, h = lax.axis_index("z"), lax.axis_index("xh")
-    here = jnp.stack([z, h]).astype(jnp.int32)
-
-    planes, spots = [], []
-    for zz in range(8):
-        for xl in range(2):
-            for yy in range(4):
-                to = 4 * xl + yy
-                spot = (to - zz) % 8
-                at = zz * 8 + xl * 4 + yy
-                planes.append((at, zz * 8 + spot))
-                spots.append((zz * 8 + spot, to * 8 + spot))
-    moved = lax.ppermute(out_grad, ("z", "xl", "y"), planes)
-    moved = lax.ppermute(moved, ("z", "xl", "y"), spots)
-    other_weight = lax.ppermute(out_weight, "xh", SWAP)
-    og = lax.all_gather(moved, FSDP, axis=0).reshape(8, 2, 128, 512)
-
-    chunks = pl.pallas_call(pack_kernel, out_shape=shape((NK, 96, 128), BF16), in_specs=[VMEM], out_specs=VMEM)(projections)
+
+
+def call(kernel, **settings):
+    def run(*args):
+        return pl.pallas_call(kernel, **settings)(*args)
+
+    return run
+
+
+def compute(out_grad, out_weight, projections, short_filters, residues, decay_rates):
+    z, h, xl, spot_y, core = (lax.axis_index(a) for a in CTX + FSDP)
+    here = jnp.stack([z, h, core, 4 * xl + spot_y, 2 * z + h]).astype(jnp.int32)
+
+    route = [
+        (zz * 8 + at, at * 8 + (at - zz) % 8) for zz in range(8) for at in range(8)
+    ]
+    moved = lax.ppermute(out_grad, ("z", "xl", "y"), route)
+
+    def flip(value, axis, by):
+        return lax.ppermute(value, axis, [(i, i ^ by) for i in range(lax.axis_size(axis))])
+
+    across = flip(moved, "xl", 1)
+    near, wrap = flip(moved, "y", 1), flip(moved, "y", 3)
+    near2, wrap2 = flip(across, "y", 1), flip(across, "y", 3)
+    far, far2 = flip(wrap, "y", 1), flip(near2, "y", 3)
+    mine1 = jnp.stack([moved, across, near, wrap])
+    mine2 = jnp.stack([near2, wrap2, far, far2])
+    theirs1, theirs2 = flip(mine1, "core", 1), flip(mine2, "core", 1)
+    other_weight = flip(out_weight, "xh", 1)
+
+    chunks, prm = call(
+        pack_kernel,
+        out_shape=(shape((NK, 96, 128), BF16), shape((56, 128))),
+        in_specs=[pl.BlockSpec(memory_space=pltpu.SMEM)] + [VMEM] * 4,
+        out_specs=(VMEM, VMEM),
+    )(here[4:], projections, residues, decay_rates, short_filters)
     x = lax.all_to_all(chunks, CTX, 0, 0)
-    prm = jnp.concatenate([residues, decay_rates, short_filters.reshape(9, 512)], axis=0)
-    prm = lax.dynamic_slice(prm, (0, (2 * z + h) * SUB), (41, SUB))
-    prm = jnp.pad(jnp.tile(prm, (1, 4)), ((0, 7), (0, 0)))
-
-    keep, send, state_in = pl.pallas_call(
+
+    smem = pl.BlockSpec(memory_space=pltpu.SMEM)
+    keep, send, state_in = call(
         forward_kernel,
         out_shape=(shape((8, STEPS, 128), BF16), shape((8, STEPS, 128), BF16), shape((NM * NK, 128))),
-        in_specs=[pl.BlockSpec(memory_space=pltpu.SMEM), VMEM, VMEM],
-        out_specs=(VMEM, VMEM, VMEM),
+        in_specs=[smem, VMEM, VMEM],
+        out_specs=(VMEM,) * 3,
         scratch_shapes=SCANS + [scratch(ROWS, 128)],
         compiler_params=PARAMS,
-    )(here[1:], x, prm)
-    y = lax.all_gather(jnp.stack([keep, lax.ppermute(send, "xh", SWAP)]), "z", axis=0)
-
-    parts = pl.pallas_call(
-        partial_kernel,
-        out_shape=shape((NK, 8, STEPS, 128), BF16),
-        grid_spec=pltpu.PrefetchScalarGridSpec(
-            num_scalar_prefetch=1,
-            grid=(8,),
-            in_specs=[
-                pl.BlockSpec((1, 2, 128, 512), lambda p, at: (p, 0, 0, 0)),
-                pl.BlockSpec((512, 512), lambda p, at: (0, 0)),
-                pl.BlockSpec((512, 512), lambda p, at: (0, 0)),
-            ],
-            out_specs=pl.BlockSpec((NK, 1, STEPS, 128), lambda p, at: (0, (at[0] - p + 8) % 8, 0, 0)),
-        ),
-        compiler_params=PARAMS,
-    )(here, og, out_weight, other_weight)
-    grad_y = lax.all_to_all(parts, CTX, 0, 0).reshape(8, 2, 8, STEPS, 128)
-
-    out = pl.pallas_call(
+    )(here, x, prm)
+
+    def turn(value, by):
+        return lax.ppermute(value, "z", [(i, (i + by) % 8) for i in range(8)])
+
+    y0 = jnp.stack([keep, flip(send, "xh", 1)])
+    r1, l1 = turn(y0, 1), turn(y0, -1)
+    r2, l2 = turn(r1, 1), turn(l1, -1)
+    r3, l3 = turn(r2, 1), turn(l2, -1)
+    r4 = turn(r2, 2)
+
+    grads, rows, after = [], [], state_in
+    for mine, theirs in ((mine1, theirs1), (mine2, theirs2)):
+        parts, blocks = call(
+            partial_kernel,
+            out_shape=(shape((NK, 4, STEPS, 128), BF16), shape((2, 512, 512), BF16)),
+            in_specs=[smem] + [VMEM] * 4 + [pl.BlockSpec(memory_space=pl.ANY)],
+            out_specs=(VMEM, VMEM),
+            compiler_params=PARAMS,
+        )(here, mine, theirs, out_weight, other_weight, after)
+        grads.append(lax.all_to_all(parts, CTX, 0, 0))
+        rows.append(blocks)
+
+    out = call(
         backward_kernel,
         out_shape=shape((NK, 128, 128), BF16),
-        in_specs=[VMEM] * 4,
+        in_specs=[smem] + [VMEM] * 5,
         out_specs=VMEM,
         scratch_shapes=SCANS
         + [scratch(ROWS, 128)] * 3
         + [scratch(NM, ROWS + NK, 128), scratch(ROWS, 128), scratch(3, ROWS + 2 * NK, 128)]
         + [scratch(3 * ROWS, 128), scratch(48 * 8, 128), scratch(32, 128)],
         compiler_params=PARAMS,
-    )(x, prm, state_in, grad_y)
+    )(here, x, prm, state_in, *grads)
     back = lax.all_to_all(out, CTX, 0, 0)
-    grad_projections, grad_short, grad_res, grad_rate = pl.pallas_call(
+    grad_projections, grad_short, grad_res, grad_rate = call(
         unpack_kernel,
         out_shape=(shape((3, 128, 512), BF16), shape((3, 3, 512)), shape((NM, 512)), shape((NM, 512))),
         in_specs=[VMEM],
@@ -429,22 +474,15 @@
         scratch_shapes=[scratch(48, 512)],
     )(back)
 
-    own, send = pl.pallas_call(
+    own, send = call(
         weight_kernel,
         out_shape=(shape((512, 512)), shape((512, 512), BF16)),
-        grid_spec=pltpu.PrefetchScalarGridSpec(
-            num_scalar_prefetch=1,
-            grid=(8,),
-            in_specs=[
-                pl.BlockSpec((1, 2, 128, 512), lambda p, at: (p, 0, 0, 0)),
-                pl.BlockSpec((8, 2, 1, STEPS, 128), lambda p, at: (0, 0, (at[0] - p + 8) % 8, 0, 0)),
-            ],
-            out_specs=[pl.BlockSpec((512, 512), lambda p, at: (0, 0))] * 2,
-            scratch_shapes=[scratch(512, 512), pltpu.VMEM((128, 512), BF16)],
-        ),
+        in_specs=[smem] + [VMEM] * 10,
+        out_specs=(VMEM, VMEM),
+        scratch_shapes=[pltpu.VMEM((8, 2, 8, STEPS, 128), BF16), pltpu.VMEM((1024, 512), BF16)],
         compiler_params=PARAMS,
-    )(here, og, y)
-    grad_weight = (own + lax.ppermute(send, "xh", SWAP).astype(F32)).astype(BF16)
+    )(here, *rows, y0, r1, r2, r3, r4, l3, l2, l1)
+    grad_weight = (own + flip(send, "xh", 1).astype(F32)).astype(BF16)
     return grad_weight, grad_projections, grad_short, grad_res, grad_rate
 
 
@@ -459,7 +497,7 @@
         P(None, FSDP),
     )
     return jax.shard_map(
-        on_device,
+        compute,
         mesh=fine,
         in_specs=placed,
         out_specs=(

time: 186 us -> 173 us (0.930); the launches traced: 185 us -> 171 us
  starting transfers between devices: 45 us -> 71.3 us
  waiting for transfers between devices: 85.3 us -> 70.3 us
  between operations: 15.6 us -> 0.81 us
  local copies, waits for them, and re-layouts: 12.2 us -> 6.03 us
  Pallas kernels: 25.6 us -> 21 us
    all_gather x2 -> x0, waiting for transfers between devices: 33.8 us -> none  [the longest x1 19.5 us: on_device(): lax.all_gather(jnp.stack([keep, lax.ppermute(send, 'xh', SWAP)]), 'z', ax...]
    ppermute x5 -> x20, waiting for transfers between devices: 34.3 us -> 57.8 us  [the longest x7 24.3 us: turn(): return lax.ppermute(value, 'z', [(i, (i + by) % 8) for i in range(8)])]
    ppermute x5 -> x20, starting transfers between devices: 24.9 us -> 38.2 us  [the longest x12 20.4 us: flip(): lax.ppermute(value, axis, [(i, i ^ by) for i in range(lax.axis_size(axis))])]
    all_to_all x3 -> x4, starting transfers between devices: 20 us -> 33.1 us  [the longest x2 16.7 us: compute(): grads.append(lax.all_to_all(parts, CTX, 0, 0))]
    all_to_all x3 -> x4, waiting for transfers between devices: 17.2 us -> 12.5 us  [the longest x1 11.7 us: compute(): x = lax.all_to_all(chunks, CTX, 0, 0)]
    pallas_call x6 -> x7, Pallas kernels: 25.6 us -> 21 us  [run(): return pl.pallas_call(kernel, **settings)(*args)]
    unnamed x28 -> x20, local copies, waits for them, and re-layouts: 9.01 us -> 5.94 us
    another operation x2 -> x1, local copies, waits for them, and re-layouts: 2.4 us -> 0.09 us  [compute(): here = jnp.stack([z, h, core, 4 * xl + spot_y, 2 * z + h]).astype(jnp.int32)]
  transfers between devices with their start and end apart: 10 -> 24, of which waited for: 7 -> 13; matrix products, arithmetic and copies ran while one was open for 3% -> 1% of each run, Pallas kernels for 12% -> 10%
where the time goes in v2:
time: 173 us; the launch traced here: 171 us
  starting transfers between devices  71.3 us (41%)
  waiting for transfers between devices  70.3 us (41%)
  Pallas kernels  21 us (12%)
  local copies, waits for them, and re-layouts  6.03 us (3%)
    ppermute x7, waiting for transfers between devices, turn(): return lax.ppermute(value, 'z', [(i, (i + by) % 8) for i in range(8)])  24.3 us
    pallas_call x7, Pallas kernels, run(): return pl.pallas_call(kernel, **settings)(*args)  21 us
    ppermute x12, waiting for transfers between devices, flip(): lax.ppermute(value, axis, [(i, i ^ by) for i in range(lax.axis_size(axis))])  20.6 us
    ppermute x12, starting transfers between devices, flip(): lax.ppermute(value, axis, [(i, i ^ by) for i in range(lax.axis_size(axis))])  20.4 us
    all_to_all x2, starting transfers between devices, compute(): grads.append(lax.all_to_all(parts, CTX, 0, 0))  16.7 us
    ppermute x1, waiting for transfers between devices, compute(): moved = lax.ppermute(out_grad, ('z', 'xl', 'y'), route)  12.9 us
    ppermute x7, starting transfers between devices, turn(): return lax.ppermute(value, 'z', [(i, (i + by) % 8) for i in range(8)])  12.7 us
    all_to_all x1, waiting for transfers between devices, compute(): x = lax.all_to_all(chunks, CTX, 0, 0)  11.7 us
  transfers between devices with their start and end apart: 24, of which 13 were waited for; matrix products, arithmetic and copies ran while one was open for 1% of the time, Pallas kernels for 10%

profile of v2, /device:TPU:16, one launch (start us, length us, event | category | flops | bytes accessed | tf_op | source)
XLA Modules:
  0.0 170.6 jit_solution(1250720821804907240)
XLA Ops:
  0.6 5.2 %collective-permute-start = (bf16[128,512]{1,0:T(8,128)(2,1)}, bf16[128,512]{1,0:T(8,128)(2,1)S(1)}, u32[]{:S(2)}, u32[]{:S(2)}) collective-permute-start(bf16[128,512]{1,0:T(8,128)(2,1)} %param.6), channel_id=1, source_target_pairs={{0,0},{2,34},{4,68},{6,102},{8,136},{10,170},{12,204},{14,238},{32... | collective-permute-start | bytes 393224 | tf_op jit(solution)/shard_map/ppermute | solution.py:404
  5.8 12.9 %collective-permute-done = bf16[128,512]{1,0:T(8,128)(2,1)S(1)} collective-permute-done((bf16[128,512]{1,0:T(8,128)(2,1)}, bf16[128,512]{1,0:T(8,128)(2,1)S(1)}, u32[]{:S(2)}, u32[]{:S(2)}) %collective-permute-start) | collective-permute-done | bytes 131104 | tf_op jit(solution)/shard_map/ppermute | solution.py:404
  22.7 2.3 %shard_map.101 = (bf16[16,96,128]{2,1,0:T(8,128)(2,1)}, f32[56,128]{1,0:T(8,128)}) custom-call(s32[1]{0:T(128)} %bitcast.4.at_ref, bf16[3,128,512]{2,1,0:T(8,128)(2,1)} %x_ref.1, f32[16,512]{1,0:T(8,128)} %res_ref.1, f32[16,512]{1,0:T(8,128)} %rate_ref.1, f32[3,3,512]{2,1,0:T(4,128)} %tap_ref.1), custom_call_target="tpu_custom_call" | custom-call | tf_op jit(solution)/shard_map/pallas_call | solution.py:392
  24.9 9.2 %all-to-all-start = ((bf16[16,96,128]{2,1,0:T(8,128)(2,1)}), bf16[16,96,128]{2,1,0:T(8,128)(2,1)S(1)}, u32[]{:S(2)}, u32[]{:S(2)}) async-start(bf16[16,96,128]{2,1,0:T(8,128)(2,1)} %get-tuple-element.20), calls=%async_computation | async-start | bytes 786432 | tf_op jit(solution)/shard_map/all_to_all | solution.py:424
  34.2 3.5 %collective-permute-start.5 = (bf16[512,512]{1,0:T(8,128)(2,1)S(1)}, bf16[512,512]{1,0:T(8,128)(2,1)S(1)}, u32[]{:S(2)}, u32[]{:S(2)}) collective-permute-start(bf16[512,512]{1,0:T(8,128)(2,1)S(1)} %copy-done), channel_id=1, source_target_pairs={{0,16},{16,0},{1,17},{17,1},{2,18},{18,2},{3,19},{19,3},{4,20},{20... | collective-permute-start | bytes 1572872 | tf_op jit(solution)/shard_map/ppermute | solution.py:407
  38.0 11.7 %all-to-all-done.x_ref = bf16[16,96,128]{2,1,0:T(8,128)(2,1)S(1)} async-done(((bf16[16,96,128]{2,1,0:T(8,128)(2,1)}), bf16[16,96,128]{2,1,0:T(8,128)(2,1)S(1)}, u32[]{:S(2)}, u32[]{:S(2)}) %all-to-all-start) | async-done | bytes 393248 | tf_op jit(solution)/shard_map/all_to_all | solution.py:424
  49.7 2.8 %shard_map.102 = (bf16[8,32,128]{2,1,0:T(8,128)(2,1)S(1)}, bf16[8,32,128]{2,1,0:T(8,128)(2,1)S(1)}, f32[256,128]{1,0:T(8,128)S(1)}) custom-call(s32[5]{0:T(128)S(1)} %stack.62.at_ref, bf16[16,96,128]{2,1,0:T(8,128)(2,1)S(1)} %all-to-all-done.x_ref, f32[56,128]{1,0:T(8,128)S(1)} %copy-done.7), custom_call_target="tpu_custom_call" | custom-call | tf_op jit(solution)/shard_map/pallas_call | solution.py:392
  56.9 8.3 %all-to-all-start.1 = ((bf16[16,4,32,128]{3,2,1,0:T(8,128)(2,1)}), bf16[16,4,32,128]{3,2,1,0:T(8,128)(2,1)S(1)}, u32[]{:S(2)}, u32[]{:S(2)}) async-start(bf16[16,4,32,128]{3,2,1,0:T(8,128)(2,1)} %copy-done.5), calls=%async_computation.1 | async-start | bytes 1048576 | tf_op jit(solution)/shard_map/all_to_all | solution.py:454
  67.9 2.3 %collective-permute-start.8 = (bf16[128,512]{1,0:T(8,128)(2,1)S(1)}, bf16[128,512]{1,0:T(8,128)(2,1)S(1)}, u32[]{:S(2)}, u32[]{:S(2)}) collective-permute-start(bf16[128,512]{1,0:T(8,128)(2,1)S(1)} %collective-permute-done.3), channel_id=1, source_target_pairs={{0,2},{2,0},{4,6},{6,4},{1,3},{3,1},{5,7},{7,5},{8,10},{10,8},{12,... | collective-permute-start | bytes 393224 | tf_op jit(solution)/shard_map/ppermute | solution.py:407
  73.2 3.2 %collective-permute-done.9 = bf16[128,512]{1,0:T(8,128)(2,1)S(1)} collective-permute-done((bf16[128,512]{1,0:T(8,128)(2,1)S(1)}, bf16[128,512]{1,0:T(8,128)(2,1)S(1)}, u32[]{:S(2)}, u32[]{:S(2)}) %collective-permute-start.9) | collective-permute-done | bytes 131104 | tf_op jit(solution)/shard_map/ppermute | solution.py:407
  82.6 8.4 %all-to-all-start.2 = ((bf16[16,4,32,128]{3,2,1,0:T(8,128)(2,1)}), bf16[16,4,32,128]{3,2,1,0:T(8,128)(2,1)S(1)}, u32[]{:S(2)}, u32[]{:S(2)}) async-start(bf16[16,4,32,128]{3,2,1,0:T(8,128)(2,1)} %copy-done.6), calls=%async_computation.2 | async-start | bytes 1048576 | tf_op jit(solution)/shard_map/all_to_all | solution.py:454
  91.1 3.4 %collective-permute-start.11 = (bf16[8,32,128]{2,1,0:T(8,128)(2,1)S(1)}, bf16[8,32,128]{2,1,0:T(8,128)(2,1)S(1)}, u32[]{:S(2)}, u32[]{:S(2)}) collective-permute-start(bf16[8,32,128]{2,1,0:T(8,128)(2,1)S(1)} %get-tuple-element.26), channel_id=1, source_target_pairs={{0,16},{16,0},{1,17},{17,1},{2,18},{18,2},{3,19},{19,3},{4,20},{20... | collective-permute-start | bytes 196616 | tf_op jit(solution)/shard_map/ppermute | solution.py:407
  94.5 2.8 %collective-permute-done.11 = bf16[8,32,128]{2,1,0:T(8,128)(2,1)S(1)} collective-permute-done((bf16[8,32,128]{2,1,0:T(8,128)(2,1)S(1)}, bf16[8,32,128]{2,1,0:T(8,128)(2,1)S(1)}, u32[]{:S(2)}, u32[]{:S(2)}) %collective-permute-start.11) | collective-permute-done | bytes 65568 | tf_op jit(solution)/shard_map/ppermute | solution.py:407
  100.6 8.2 %collective-permute-done.12.r1 = bf16[2,8,32,128]{3,2,1,0:T(8,128)(2,1)S(1)} collective-permute-done((bf16[2,8,32,128]{3,2,1,0:T(8,128)(2,1)S(1)}, bf16[2,8,32,128]{3,2,1,0:T(8,128)(2,1)S(1)}, u32[]{:S(2)}, u32[]{:S(2)}) %collective-permute-start.12) | collective-permute-done | bytes 131104 | tf_op jit(solution)/shard_map/ppermute | solution.py:437
  108.9 3.2 %collective-permute-start.17 = (bf16[2,8,32,128]{3,2,1,0:T(8,128)(2,1)S(1)}, bf16[2,8,32,128]{3,2,1,0:T(8,128)(2,1)}, u32[]{:S(2)}, u32[]{:S(2)}) collective-permute-start(bf16[2,8,32,128]{3,2,1,0:T(8,128)(2,1)S(1)} %collective-permute-done.16.l1), channel_id=1, source_target_pairs={{0,224},{32,0},{64,32},{96,64},{128,96},{160,128},{192,160},{224,1... | collective-permute-start | bytes 393224 | tf_op jit(solution)/shard_map/ppermute | solution.py:437
  112.9 6.7 %shard_map.106 = bf16[16,128,128]{2,1,0:T(8,128)(2,1)} custom-call(s32[5]{0:T(128)S(1)} %stack.62.at_ref, bf16[16,96,128]{2,1,0:T(8,128)(2,1)S(1)} %all-to-all-done.x_ref, f32[56,128]{1,0:T(8,128)S(1)} %copy-done.8, f32[256,128]{1,0:T(8,128)S(1)} %get-tuple-element.22.after_ref.in_ref, bf16[16,4,32,128]{3,2,1,0:T(8,128)(2,1)S(1)} %all-to-all-done.1.gy1_ref, ...), custom_call_target="tpu_custom_call" | custom-call | tf_op jit(solution)/shard_map/pallas_call | solution.py:392
  119.5 7.2 %all-to-all-start.3 = ((bf16[16,128,128]{2,1,0:T(8,128)(2,1)}), bf16[16,128,128]{2,1,0:T(8,128)(2,1)S(1)}, u32[]{:S(2)}, u32[]{:S(2)}) async-start(bf16[16,128,128]{2,1,0:T(8,128)(2,1)} %shard_map.106), calls=%async_computation.3 | async-start | bytes 1048576 | tf_op jit(solution)/shard_map/all_to_all | solution.py:468
  128.7 2.4 %collective-permute-start.15 = (bf16[2,8,32,128]{3,2,1,0:T(8,128)(2,1)}, bf16[2,8,32,128]{3,2,1,0:T(8,128)(2,1)S(1)}, u32[]{:S(2)}, u32[]{:S(2)}) collective-permute-start(bf16[2,8,32,128]{3,2,1,0:T(8,128)(2,1)} %collective-permute-done.13.r2), channel_id=1, source_target_pairs={{0,64},{32,96},{64,128},{96,160},{128,192},{160,224},{192,0},{224,... | collective-permute-start | bytes 393224 | tf_op jit(solution)/shard_map/ppermute | solution.py:437
  132.9 12.7 %collective-permute-done.14.r3 = bf16[2,8,32,128]{3,2,1,0:T(8,128)(2,1)S(1)} collective-permute-done((bf16[2,8,32,128]{3,2,1,0:T(8,128)(2,1)}, bf16[2,8,32,128]{3,2,1,0:T(8,128)(2,1)S(1)}, u32[]{:S(2)}, u32[]{:S(2)}) %collective-permute-start.14) | collective-permute-done | bytes 131104 | tf_op jit(solution)/shard_map/ppermute | solution.py:437
  145.5 3.4 %collective-permute-done.15.r4 = bf16[2,8,32,128]{3,2,1,0:T(8,128)(2,1)S(1)} collective-permute-done((bf16[2,8,32,128]{3,2,1,0:T(8,128)(2,1)}, bf16[2,8,32,128]{3,2,1,0:T(8,128)(2,1)S(1)}, u32[]{:S(2)}, u32[]{:S(2)}) %collective-permute-start.15) | collective-permute-done | bytes 131104 | tf_op jit(solution)/shard_map/ppermute | solution.py:437
  148.9 3.1 %shard_map.105 = (f32[512,512]{1,0:T(8,128)S(1)}, bf16[512,512]{1,0:T(8,128)(2,1)S(1)}) custom-call(s32[5]{0:T(128)S(1)} %stack.62.at_ref, bf16[2,512,512]{2,1,0:T(8,128)(2,1)S(1)} %get-tuple-element.23.rows1_ref, bf16[2,512,512]{2,1,0:T(8,128)(2,1)S(1)} %copy-done.2, bf16[2,8,32,128]{3,2,1,0:T(8,128)(2,1)S(1)} %pad_maximum_fusion.2.y0, ...), custom_call_target="tpu_custom_call" | custom-call | tf_op jit(solution)/shard_map/pallas_call | solution.py:392
  152.1 3.1 %collective-permute-start.19 = (bf16[512,512]{1,0:T(8,128)(2,1)S(1)}, bf16[512,512]{1,0:T(8,128)(2,1)S(1)}, u32[]{:S(2)}, u32[]{:S(2)}) collective-permute-start(bf16[512,512]{1,0:T(8,128)(2,1)S(1)} %get-tuple-element.28), channel_id=1, source_target_pairs={{0,16},{16,0},{1,17},{17,1},{2,18},{18,2},{3,19},{19,3},{4,20},{20... | collective-permute-start | bytes 1572872 | tf_op jit(solution)/shard_map/ppermute | solution.py:407
  155.1 10.6 %collective-permute-done.19 = bf16[512,512]{1,0:T(8,128)(2,1)S(1)} collective-permute-done((bf16[512,512]{1,0:T(8,128)(2,1)S(1)}, bf16[512,512]{1,0:T(8,128)(2,1)S(1)}, u32[]{:S(2)}, u32[]{:S(2)}) %collective-permute-start.19) | collective-permute-done | bytes 524320 | tf_op jit(solution)/shard_map/ppermute | solution.py:407
  167.5 3.1 %shard_map.107 = (bf16[3,128,512]{2,1,0:T(8,128)(2,1)}, f32[3,3,512]{2,1,0:T(4,128)}, f32[16,512]{1,0:T(8,128)}, f32[16,512]{1,0:T(8,128)}) custom-call(bf16[16,128,128]{2,1,0:T(8,128)(2,1)} %copy-done.9), custom_call_target="tpu_custom_call" | custom-call | tf_op jit(solution)/shard_map/pallas_call | solution.py:392
  (56 shorter events, 30.1 us)
Async XLA Ops:
  0.6 18.1 %collective-permute-start = (bf16[128,512]{1,0:T(8,128)(2,1)}, bf16[128,512]{1,0:T(8,128)(2,1)S(1)}, u32[]{:S(2)}, u32[]{:S(2)}) collective-permute-start(bf16[128,512]{1,0:T(8,128)(2,1)} %param.6), channel_id=1, source_target_pairs={{0,0},{2,34},{4,68},{6,102},{8,136},{10,170},{12,204},{14,238},{32... | collective-permute-start | bytes 393224 | tf_op jit(solution)/shard_map/ppermute | solution.py:404
  18.7 19.0 %collective-permute-start.1 = (bf16[128,512]{1,0:T(8,128)(2,1)S(1)}, bf16[128,512]{1,0:T(8,128)(2,1)S(1)}, u32[]{:S(2)}, u32[]{:S(2)}) collective-permute-start(bf16[128,512]{1,0:T(8,128)(2,1)S(1)} %collective-permute-done), channel_id=1, source_target_pairs={{0,8},{8,0},{1,9},{9,1},{2,10},{10,2},{3,11},{11,3},{4,12},{12,4},... | collective-permute-start | bytes 393224 | tf_op jit(solution)/shard_map/ppermute | solution.py:407
  18.7 18.9 %collective-permute-start.3 = (bf16[128,512]{1,0:T(8,128)(2,1)S(1)}, bf16[128,512]{1,0:T(8,128)(2,1)S(1)}, u32[]{:S(2)}, u32[]{:S(2)}) collective-permute-start(bf16[128,512]{1,0:T(8,128)(2,1)S(1)} %collective-permute-done), channel_id=1, source_target_pairs={{0,6},{2,4},{4,2},{6,0},{1,7},{3,5},{5,3},{7,1},{8,14},{10,12},{12... | collective-permute-start | bytes 393224 | tf_op jit(solution)/shard_map/ppermute | solution.py:407
  20.9 16.8 %collective-permute-start.2 = (bf16[128,512]{1,0:T(8,128)(2,1)S(1)}, bf16[128,512]{1,0:T(8,128)(2,1)S(1)}, u32[]{:S(2)}, u32[]{:S(2)}) collective-permute-start(bf16[128,512]{1,0:T(8,128)(2,1)S(1)} %collective-permute-done), channel_id=1, source_target_pairs={{0,2},{2,0},{4,6},{6,4},{1,3},{3,1},{5,7},{7,5},{8,10},{10,8},{12,... | collective-permute-start | bytes 393224 | tf_op jit(solution)/shard_map/ppermute | solution.py:407
  24.9 24.7 %all-to-all-start = ((bf16[16,96,128]{2,1,0:T(8,128)(2,1)}), bf16[16,96,128]{2,1,0:T(8,128)(2,1)S(1)}, u32[]{:S(2)}, u32[]{:S(2)}) async-start(bf16[16,96,128]{2,1,0:T(8,128)(2,1)} %get-tuple-element.20), calls=%async_computation | async-start | bytes 786432 | tf_op jit(solution)/shard_map/all_to_all | solution.py:424
  34.2 18.6 %collective-permute-start.5 = (bf16[512,512]{1,0:T(8,128)(2,1)S(1)}, bf16[512,512]{1,0:T(8,128)(2,1)S(1)}, u32[]{:S(2)}, u32[]{:S(2)}) collective-permute-start(bf16[512,512]{1,0:T(8,128)(2,1)S(1)} %copy-done), channel_id=1, source_target_pairs={{0,16},{16,0},{1,17},{17,1},{2,18},{18,2},{3,19},{19,3},{4,20},{20... | collective-permute-start | bytes 1572872 | tf_op jit(solution)/shard_map/ppermute | solution.py:407
  37.8 15.0 %collective-permute-start.4 = (bf16[4,128,512]{2,1,0:T(8,128)(2,1)S(1)}, bf16[4,128,512]{2,1,0:T(8,128)(2,1)S(1)}, u32[]{:S(2)}, u32[]{:S(2)}) collective-permute-start(bf16[4,128,512]{2,1,0:T(8,128)(2,1)S(1)} %pad_maximum_fusion.mine_ref), channel_id=1, source_target_pairs={{0,1},{1,0},{2,3},{3,2},{4,5},{5,4},{6,7},{7,6},{8,9},{9,8},{10,11... | collective-permute-start | bytes 1572872 | tf_op jit(solution)/shard_map/ppermute | solution.py:407
  56.9 25.7 %all-to-all-start.1 = ((bf16[16,4,32,128]{3,2,1,0:T(8,128)(2,1)}), bf16[16,4,32,128]{3,2,1,0:T(8,128)(2,1)S(1)}, u32[]{:S(2)}, u32[]{:S(2)}) async-start(bf16[16,4,32,128]{3,2,1,0:T(8,128)(2,1)} %copy-done.5), calls=%async_computation.1 | async-start | bytes 1048576 | tf_op jit(solution)/shard_map/all_to_all | solution.py:454
  65.2 6.2 %collective-permute-start.6 = (bf16[128,512]{1,0:T(8,128)(2,1)S(1)}, bf16[128,512]{1,0:T(8,128)(2,1)S(1)}, u32[]{:S(2)}, u32[]{:S(2)}) collective-permute-start(bf16[128,512]{1,0:T(8,128)(2,1)S(1)} %collective-permute-done.1), channel_id=1, source_target_pairs={{0,2},{2,0},{4,6},{6,4},{1,3},{3,1},{5,7},{7,5},{8,10},{10,8},{12,... | collective-permute-start | bytes 393224 | tf_op jit(solution)/shard_map/ppermute | solution.py:407
  65.7 6.9 %collective-permute-start.7 = (bf16[128,512]{1,0:T(8,128)(2,1)S(1)}, bf16[128,512]{1,0:T(8,128)(2,1)S(1)}, u32[]{:S(2)}, u32[]{:S(2)}) collective-permute-start(bf16[128,512]{1,0:T(8,128)(2,1)S(1)} %collective-permute-done.1), channel_id=1, source_target_pairs={{0,6},{2,4},{4,2},{6,0},{1,7},{3,5},{5,3},{7,1},{8,14},{10,12},{12... | collective-permute-start | bytes 393224 | tf_op jit(solution)/shard_map/ppermute | solution.py:407
  67.9 5.3 %collective-permute-start.8 = (bf16[128,512]{1,0:T(8,128)(2,1)S(1)}, bf16[128,512]{1,0:T(8,128)(2,1)S(1)}, u32[]{:S(2)}, u32[]{:S(2)}) collective-permute-start(bf16[128,512]{1,0:T(8,128)(2,1)S(1)} %collective-permute-done.3), channel_id=1, source_target_pairs={{0,2},{2,0},{4,6},{6,4},{1,3},{3,1},{5,7},{7,5},{8,10},{10,8},{12,... | collective-permute-start | bytes 393224 | tf_op jit(solution)/shard_map/ppermute | solution.py:407
  71.5 5.0 %collective-permute-start.9 = (bf16[128,512]{1,0:T(8,128)(2,1)S(1)}, bf16[128,512]{1,0:T(8,128)(2,1)S(1)}, u32[]{:S(2)}, u32[]{:S(2)}) collective-permute-start(bf16[128,512]{1,0:T(8,128)(2,1)S(1)} %collective-permute-done.6), channel_id=1, source_target_pairs={{0,6},{2,4},{4,2},{6,0},{1,7},{3,5},{5,3},{7,1},{8,14},{10,12},{12... | collective-permute-start | bytes 393224 | tf_op jit(solution)/shard_map/ppermute | solution.py:407
  76.5 2.0 %collective-permute-start.10 = (bf16[4,128,512]{2,1,0:T(8,128)(2,1)S(1)}, bf16[4,128,512]{2,1,0:T(8,128)(2,1)S(1)}, u32[]{:S(2)}, u32[]{:S(2)}) collective-permute-start(bf16[4,128,512]{2,1,0:T(8,128)(2,1)S(1)} %pad_maximum_fusion.1.mine_ref), channel_id=1, source_target_pairs={{0,1},{1,0},{2,3},{3,2},{4,5},{5,4},{6,7},{7,6},{8,9},{9,8},{10,11... | collective-permute-start | bytes 1572872 | tf_op jit(solution)/shard_map/ppermute | solution.py:407
  82.6 29.5 %all-to-all-start.2 = ((bf16[16,4,32,128]{3,2,1,0:T(8,128)(2,1)}), bf16[16,4,32,128]{3,2,1,0:T(8,128)(2,1)S(1)}, u32[]{:S(2)}, u32[]{:S(2)}) async-start(bf16[16,4,32,128]{3,2,1,0:T(8,128)(2,1)} %copy-done.6), calls=%async_computation.2 | async-start | bytes 1048576 | tf_op jit(solution)/shard_map/all_to_all | solution.py:454
  91.1 6.2 %collective-permute-start.11 = (bf16[8,32,128]{2,1,0:T(8,128)(2,1)S(1)}, bf16[8,32,128]{2,1,0:T(8,128)(2,1)S(1)}, u32[]{:S(2)}, u32[]{:S(2)}) collective-permute-start(bf16[8,32,128]{2,1,0:T(8,128)(2,1)S(1)} %get-tuple-element.26), channel_id=1, source_target_pairs={{0,16},{16,0},{1,17},{17,1},{2,18},{18,2},{3,19},{19,3},{4,20},{20... | collective-permute-start | bytes 196616 | tf_op jit(solution)/shard_map/ppermute | solution.py:407
  97.3 11.6 %collective-permute-start.12 = (bf16[2,8,32,128]{3,2,1,0:T(8,128)(2,1)S(1)}, bf16[2,8,32,128]{3,2,1,0:T(8,128)(2,1)S(1)}, u32[]{:S(2)}, u32[]{:S(2)}) collective-permute-start(bf16[2,8,32,128]{3,2,1,0:T(8,128)(2,1)S(1)} %pad_maximum_fusion.2.y0), channel_id=1, source_target_pairs={{0,32},{32,64},{64,96},{96,128},{128,160},{160,192},{192,224},{224... | collective-permute-start | bytes 393224 | tf_op jit(solution)/shard_map/ppermute | solution.py:437
  99.1 9.7 %collective-permute-start.16 = (bf16[2,8,32,128]{3,2,1,0:T(8,128)(2,1)S(1)}, bf16[2,8,32,128]{3,2,1,0:T(8,128)(2,1)S(1)}, u32[]{:S(2)}, u32[]{:S(2)}) collective-permute-start(bf16[2,8,32,128]{3,2,1,0:T(8,128)(2,1)S(1)} %pad_maximum_fusion.2.y0), channel_id=1, source_target_pairs={{0,224},{32,0},{64,32},{96,64},{128,96},{160,128},{192,160},{224,1... | collective-permute-start | bytes 393224 | tf_op jit(solution)/shard_map/ppermute | solution.py:437
  108.9 17.8 %collective-permute-start.13 = (bf16[2,8,32,128]{3,2,1,0:T(8,128)(2,1)S(1)}, bf16[2,8,32,128]{3,2,1,0:T(8,128)(2,1)}, u32[]{:S(2)}, u32[]{:S(2)}) collective-permute-start(bf16[2,8,32,128]{3,2,1,0:T(8,128)(2,1)S(1)} %collective-permute-done.12.r1), channel_id=1, source_target_pairs={{0,32},{32,64},{64,96},{96,128},{128,160},{160,192},{192,224},{224... | collective-permute-start | bytes 393224 | tf_op jit(solution)/shard_map/ppermute | solution.py:437
  108.9 22.2 %collective-permute-start.17 = (bf16[2,8,32,128]{3,2,1,0:T(8,128)(2,1)S(1)}, bf16[2,8,32,128]{3,2,1,0:T(8,128)(2,1)}, u32[]{:S(2)}, u32[]{:S(2)}) collective-permute-start(bf16[2,8,32,128]{3,2,1,0:T(8,128)(2,1)S(1)} %collective-permute-done.16.l1), channel_id=1, source_target_pairs={{0,224},{32,0},{64,32},{96,64},{128,96},{160,128},{192,160},{224,1... | collective-permute-start | bytes 393224 | tf_op jit(solution)/shard_map/ppermute | solution.py:437
  119.5 47.1 %all-to-all-start.3 = ((bf16[16,128,128]{2,1,0:T(8,128)(2,1)}), bf16[16,128,128]{2,1,0:T(8,128)(2,1)S(1)}, u32[]{:S(2)}, u32[]{:S(2)}) async-start(bf16[16,128,128]{2,1,0:T(8,128)(2,1)} %shard_map.106), calls=%async_computation.3 | async-start | bytes 1048576 | tf_op jit(solution)/shard_map/all_to_all | solution.py:468
  126.7 18.8 %collective-permute-start.14 = (bf16[2,8,32,128]{3,2,1,0:T(8,128)(2,1)}, bf16[2,8,32,128]{3,2,1,0:T(8,128)(2,1)S(1)}, u32[]{:S(2)}, u32[]{:S(2)}) collective-permute-start(bf16[2,8,32,128]{3,2,1,0:T(8,128)(2,1)} %collective-permute-done.13.r2), channel_id=1, source_target_pairs={{0,32},{32,64},{64,96},{96,128},{128,160},{160,192},{192,224},{224... | collective-permute-start | bytes 393224 | tf_op jit(solution)/shard_map/ppermute | solution.py:437
  128.7 20.2 %collective-permute-start.15 = (bf16[2,8,32,128]{3,2,1,0:T(8,128)(2,1)}, bf16[2,8,32,128]{3,2,1,0:T(8,128)(2,1)S(1)}, u32[]{:S(2)}, u32[]{:S(2)}) collective-permute-start(bf16[2,8,32,128]{3,2,1,0:T(8,128)(2,1)} %collective-permute-done.13.r2), channel_id=1, source_target_pairs={{0,64},{32,96},{64,128},{96,160},{128,192},{160,224},{192,0},{224,... | collective-permute-start | bytes 393224 | tf_op jit(solution)/shard_map/ppermute | solution.py:437
  131.1 17.8 %collective-permute-start.18 = (bf16[2,8,32,128]{3,2,1,0:T(8,128)(2,1)}, bf16[2,8,32,128]{3,2,1,0:T(8,128)(2,1)S(1)}, u32[]{:S(2)}, u32[]{:S(2)}) collective-permute-start(bf16[2,8,32,128]{3,2,1,0:T(8,128)(2,1)} %collective-permute-done.17.l2), channel_id=1, source_target_pairs={{0,224},{32,0},{64,32},{96,64},{128,96},{160,128},{192,160},{224,1... | collective-permute-start | bytes 393224 | tf_op jit(solution)/shard_map/ppermute | solution.py:437
  152.1 13.6 %collective-permute-start.19 = (bf16[512,512]{1,0:T(8,128)(2,1)S(1)}, bf16[512,512]{1,0:T(8,128)(2,1)S(1)}, u32[]{:S(2)}, u32[]{:S(2)}) collective-permute-start(bf16[512,512]{1,0:T(8,128)(2,1)S(1)} %get-tuple-element.28), channel_id=1, source_target_pairs={{0,16},{16,0},{1,17},{17,1},{2,18},{18,2},{3,19},{19,3},{4,20},{20... | collective-permute-start | bytes 1572872 | tf_op jit(solution)/shard_map/ppermute | solution.py:407
  (10 other events, 58.7 us)

commit v3 on v2

--- a/solution.py
+++ b/solution.py
@@ -373,6 +373,10 @@
     return jax.ShapeDtypeStruct(dims, dtype)
 
 
+def sent(dims):
+    return pltpu.HBM(dims, BF16)
+
+
 def scratch(*dims):
     return pltpu.VMEM(dims, F32)
 
@@ -417,9 +421,9 @@
 
     chunks, prm = call(
         pack_kernel,
-        out_shape=(shape((NK, 96, 128), BF16), shape((56, 128))),
+        out_shape=(sent((NK, 96, 128)), shape((56, 128))),
         in_specs=[pl.BlockSpec(memory_space=pltpu.SMEM)] + [VMEM] * 4,
-        out_specs=(VMEM, VMEM),
+        out_specs=(pl.BlockSpec(), VMEM),
     )(here[4:], projections, residues, decay_rates, short_filters)
     x = lax.all_to_all(chunks, CTX, 0, 0)
 
@@ -446,9 +450,9 @@
     for mine, theirs in ((mine1, theirs1), (mine2, theirs2)):
         parts, blocks = call(
             partial_kernel,
-            out_shape=(shape((NK, 4, STEPS, 128), BF16), shape((2, 512, 512), BF16)),
+            out_shape=(sent((NK, 4, STEPS, 128)), sent((2, 512, 512))),
             in_specs=[smem] + [VMEM] * 4 + [pl.BlockSpec(memory_space=pl.ANY)],
-            out_specs=(VMEM, VMEM),
+            out_specs=(pl.BlockSpec(), pl.BlockSpec()),
             compiler_params=PARAMS,
         )(here, mine, theirs, out_weight, other_weight, after)
         grads.append(lax.all_to_all(parts, CTX, 0, 0))
@@ -456,9 +460,9 @@
 
     out = call(
         backward_kernel,
-        out_shape=shape((NK, 128, 128), BF16),
+        out_shape=sent((NK, 128, 128)),
         in_specs=[smem] + [VMEM] * 5,
-        out_specs=VMEM,
+        out_specs=pl.BlockSpec(),
         scratch_shapes=SCANS
         + [scratch(ROWS, 128)] * 3
         + [scratch(NM, ROWS + NK, 128), scratch(ROWS, 128), scratch(3, ROWS + 2 * NK, 128)]

time: 173 us -> 169 us (0.977)
  local copies, waits for them, and re-layouts: 6.03 us -> 0.1 us
    unnamed x20 -> x8, local copies, waits for them, and re-layouts: 5.94 us -> 0.02 us
where the time goes in v3:
time: 169 us; the launch traced here: 166 us
  waiting for transfers between devices  71.1 us (42%)
  starting transfers between devices  70.6 us (42%)
  Pallas kernels  22.6 us (13%)
    ppermute x7, waiting for transfers between devices, turn(): return lax.ppermute(value, 'z', [(i, (i + by) % 8) for i in range(8)])  24.3 us
    pallas_call x7, Pallas kernels, run(): return pl.pallas_call(kernel, **settings)(*args)  22.6 us
    ppermute x12, waiting for transfers between devices, flip(): lax.ppermute(value, axis, [(i, i ^ by) for i in range(lax.axis_size(axis))])  20.6 us
    ppermute x12, starting transfers between devices, flip(): lax.ppermute(value, axis, [(i, i ^ by) for i in range(lax.axis_size(axis))])  20.4 us
    all_to_all x2, starting transfers between devices, compute(): grads.append(lax.all_to_all(parts, CTX, 0, 0))  16 us
    ppermute x1, waiting for transfers between devices, compute(): moved = lax.ppermute(out_grad, ('z', 'xl', 'y'), route)  12.9 us
    ppermute x7, starting transfers between devices, turn(): return lax.ppermute(value, 'z', [(i, (i + by) % 8) for i in range(8)])  12.6 us
    all_to_all x1, waiting for transfers between devices, compute(): x = lax.all_to_all(chunks, CTX, 0, 0)  11.7 us
  transfers between devices with their start and end apart: 24, of which 13 were waited for; matrix products, arithmetic and copies ran while one was open for 1% of the time, Pallas kernels for 10%

profile of v3, /device:TPU:16, one launch (start us, length us, event | category | flops | bytes accessed | tf_op | source)
XLA Modules:
  0.0 166.3 jit_solution(10344252943923296115)
XLA Ops:
  0.6 5.2 %collective-permute-start = (bf16[128,512]{1,0:T(8,128)(2,1)}, bf16[128,512]{1,0:T(8,128)(2,1)S(1)}, u32[]{:S(2)}, u32[]{:S(2)}) collective-permute-start(bf16[128,512]{1,0:T(8,128)(2,1)} %param.6), channel_id=1, source_target_pairs={{0,0},{2,34},{4,68},{6,102},{8,136},{10,170},{12,204},{14,238},{32... | collective-permute-start | bytes 393224 | tf_op jit(solution)/shard_map/ppermute | solution.py:408
  5.8 12.9 %collective-permute-done = bf16[128,512]{1,0:T(8,128)(2,1)S(1)} collective-permute-done((bf16[128,512]{1,0:T(8,128)(2,1)}, bf16[128,512]{1,0:T(8,128)(2,1)S(1)}, u32[]{:S(2)}, u32[]{:S(2)}) %collective-permute-start) | collective-permute-done | bytes 131104 | tf_op jit(solution)/shard_map/ppermute | solution.py:408
  24.9 9.2 %all-to-all-start = ((bf16[16,96,128]{2,1,0:T(8,128)(2,1)}), bf16[16,96,128]{2,1,0:T(8,128)(2,1)S(1)}, u32[]{:S(2)}, u32[]{:S(2)}) async-start(bf16[16,96,128]{2,1,0:T(8,128)(2,1)} %get-tuple-element.20), calls=%async_computation | async-start | bytes 786432 | tf_op jit(solution)/shard_map/all_to_all | solution.py:428
  34.2 3.5 %collective-permute-start.5 = (bf16[512,512]{1,0:T(8,128)(2,1)S(1)}, bf16[512,512]{1,0:T(8,128)(2,1)S(1)}, u32[]{:S(2)}, u32[]{:S(2)}) collective-permute-start(bf16[512,512]{1,0:T(8,128)(2,1)S(1)} %copy-done), channel_id=1, source_target_pairs={{0,16},{16,0},{1,17},{17,1},{2,18},{18,2},{3,19},{19,3},{4,20},{20... | collective-permute-start | bytes 1572872 | tf_op jit(solution)/shard_map/ppermute | solution.py:411
  38.0 11.7 %all-to-all-done.x_ref = bf16[16,96,128]{2,1,0:T(8,128)(2,1)S(1)} async-done(((bf16[16,96,128]{2,1,0:T(8,128)(2,1)}), bf16[16,96,128]{2,1,0:T(8,128)(2,1)S(1)}, u32[]{:S(2)}, u32[]{:S(2)}) %all-to-all-start) | async-done | bytes 393248 | tf_op jit(solution)/shard_map/all_to_all | solution.py:428
  49.7 2.8 %shard_map.102 = (bf16[8,32,128]{2,1,0:T(8,128)(2,1)S(1)}, bf16[8,32,128]{2,1,0:T(8,128)(2,1)S(1)}, f32[256,128]{1,0:T(8,128)S(1)}) custom-call(s32[5]{0:T(128)S(1)} %stack.62.at_ref, bf16[16,96,128]{2,1,0:T(8,128)(2,1)S(1)} %all-to-all-done.x_ref, f32[56,128]{1,0:T(8,128)S(1)} %copy-done.3), custom_call_target="tpu_custom_call" | custom-call | tf_op jit(solution)/shard_map/pallas_call | solution.py:396
  52.8 2.5 %shard_map.103 = (bf16[16,4,32,128]{3,2,1,0:T(8,128)(2,1)}, bf16[2,512,512]{2,1,0:T(8,128)(2,1)}) custom-call(s32[5]{0:T(128)S(1)} %stack.62.at_ref, bf16[4,128,512]{2,1,0:T(8,128)(2,1)S(1)} %pad_maximum_fusion.mine_ref, bf16[4,128,512]{2,1,0:T(8,128)(2,1)S(1)} %collective-permute-done.4.theirs_ref, bf16[512,512]{1,0:T(8,128)(2,1)S(1)} %copy-done, ...), custom_call_target="tpu_custom_call" | custom-call | tf_op jit(solution)/shard_map/pallas_call | solution.py:396
  55.3 8.3 %all-to-all-start.1 = ((bf16[16,4,32,128]{3,2,1,0:T(8,128)(2,1)}), bf16[16,4,32,128]{3,2,1,0:T(8,128)(2,1)S(1)}, u32[]{:S(2)}, u32[]{:S(2)}) async-start(bf16[16,4,32,128]{3,2,1,0:T(8,128)(2,1)} %get-tuple-element.29), calls=%async_computation.1 | async-start | bytes 1048576 | tf_op jit(solution)/shard_map/all_to_all | solution.py:458
  71.6 3.2 %collective-permute-done.9 = bf16[128,512]{1,0:T(8,128)(2,1)S(1)} collective-permute-done((bf16[128,512]{1,0:T(8,128)(2,1)S(1)}, bf16[128,512]{1,0:T(8,128)(2,1)S(1)}, u32[]{:S(2)}, u32[]{:S(2)}) %collective-permute-start.9) | collective-permute-done | bytes 131104 | tf_op jit(solution)/shard_map/ppermute | solution.py:411
  76.8 2.6 %shard_map.104 = (bf16[16,4,32,128]{3,2,1,0:T(8,128)(2,1)}, bf16[2,512,512]{2,1,0:T(8,128)(2,1)}) custom-call(s32[5]{0:T(128)S(1)} %stack.62.at_ref, bf16[4,128,512]{2,1,0:T(8,128)(2,1)S(1)} %pad_maximum_fusion.1.mine_ref, bf16[4,128,512]{2,1,0:T(8,128)(2,1)S(1)} %collective-permute-done.10.theirs_ref, bf16[512,512]{1,0:T(8,128)(2,1)S(1)} %copy-done, ...), custom_call_target="tpu_custom_call" | custom-call | tf_op jit(solution)/shard_map/pallas_call | solution.py:396
  81.0 7.7 %all-to-all-start.2 = ((bf16[16,4,32,128]{3,2,1,0:T(8,128)(2,1)}), bf16[16,4,32,128]{3,2,1,0:T(8,128)(2,1)S(1)}, u32[]{:S(2)}, u32[]{:S(2)}) async-start(bf16[16,4,32,128]{3,2,1,0:T(8,128)(2,1)} %get-tuple-element.30), calls=%async_computation.2 | async-start | bytes 1048576 | tf_op jit(solution)/shard_map/all_to_all | solution.py:458
  88.7 3.4 %collective-permute-start.11 = (bf16[8,32,128]{2,1,0:T(8,128)(2,1)S(1)}, bf16[8,32,128]{2,1,0:T(8,128)(2,1)S(1)}, u32[]{:S(2)}, u32[]{:S(2)}) collective-permute-start(bf16[8,32,128]{2,1,0:T(8,128)(2,1)S(1)} %get-tuple-element.26), channel_id=1, source_target_pairs={{0,16},{16,0},{1,17},{17,1},{2,18},{18,2},{3,19},{19,3},{4,20},{20... | collective-permute-start | bytes 196616 | tf_op jit(solution)/shard_map/ppermute | solution.py:411
  92.1 2.8 %collective-permute-done.11 = bf16[8,32,128]{2,1,0:T(8,128)(2,1)S(1)} collective-permute-done((bf16[8,32,128]{2,1,0:T(8,128)(2,1)S(1)}, bf16[8,32,128]{2,1,0:T(8,128)(2,1)S(1)}, u32[]{:S(2)}, u32[]{:S(2)}) %collective-permute-start.11) | collective-permute-done | bytes 65568 | tf_op jit(solution)/shard_map/ppermute | solution.py:411
  98.3 8.3 %collective-permute-done.12.r1 = bf16[2,8,32,128]{3,2,1,0:T(8,128)(2,1)S(1)} collective-permute-done((bf16[2,8,32,128]{3,2,1,0:T(8,128)(2,1)S(1)}, bf16[2,8,32,128]{3,2,1,0:T(8,128)(2,1)S(1)}, u32[]{:S(2)}, u32[]{:S(2)}) %collective-permute-start.12) | collective-permute-done | bytes 131104 | tf_op jit(solution)/shard_map/ppermute | solution.py:441
  106.5 3.2 %collective-permute-start.17 = (bf16[2,8,32,128]{3,2,1,0:T(8,128)(2,1)S(1)}, bf16[2,8,32,128]{3,2,1,0:T(8,128)(2,1)S(1)}, u32[]{:S(2)}, u32[]{:S(2)}) collective-permute-start(bf16[2,8,32,128]{3,2,1,0:T(8,128)(2,1)S(1)} %collective-permute-done.16.l1), channel_id=1, source_target_pairs={{0,224},{32,0},{64,32},{96,64},{128,96},{160,128},{192,160},{224,1... | collective-permute-start | bytes 393224 | tf_op jit(solution)/shard_map/ppermute | solution.py:441
  109.8 6.7 %shard_map.106 = bf16[16,128,128]{2,1,0:T(8,128)(2,1)} custom-call(s32[5]{0:T(128)S(1)} %stack.62.at_ref, bf16[16,96,128]{2,1,0:T(8,128)(2,1)S(1)} %all-to-all-done.x_ref, f32[56,128]{1,0:T(8,128)S(1)} %copy-done.3, f32[256,128]{1,0:T(8,128)S(1)} %get-tuple-element.22.after_ref.in_ref, bf16[16,4,32,128]{3,2,1,0:T(8,128)(2,1)S(1)} %all-to-all-done.1.gy1_ref, ...), custom_call_target="tpu_custom_call" | custom-call | tf_op jit(solution)/shard_map/pallas_call | solution.py:396
  116.4 7.2 %all-to-all-start.3 = ((bf16[16,128,128]{2,1,0:T(8,128)(2,1)}), bf16[16,128,128]{2,1,0:T(8,128)(2,1)}, u32[]{:S(2)}, u32[]{:S(2)}) async-start(bf16[16,128,128]{2,1,0:T(8,128)(2,1)} %shard_map.106), calls=%async_computation.3 | async-start | bytes 1048576 | tf_op jit(solution)/shard_map/all_to_all | solution.py:472
  125.6 2.4 %collective-permute-start.15 = (bf16[2,8,32,128]{3,2,1,0:T(8,128)(2,1)S(1)}, bf16[2,8,32,128]{3,2,1,0:T(8,128)(2,1)S(1)}, u32[]{:S(2)}, u32[]{:S(2)}) collective-permute-start(bf16[2,8,32,128]{3,2,1,0:T(8,128)(2,1)S(1)} %collective-permute-done.13.r2), channel_id=1, source_target_pairs={{0,64},{32,96},{64,128},{96,160},{128,192},{160,224},{192,0},{224,... | collective-permute-start | bytes 393224 | tf_op jit(solution)/shard_map/ppermute | solution.py:441
  129.7 12.7 %collective-permute-done.14.r3 = bf16[2,8,32,128]{3,2,1,0:T(8,128)(2,1)S(1)} collective-permute-done((bf16[2,8,32,128]{3,2,1,0:T(8,128)(2,1)S(1)}, bf16[2,8,32,128]{3,2,1,0:T(8,128)(2,1)S(1)}, u32[]{:S(2)}, u32[]{:S(2)}) %collective-permute-start.14) | collective-permute-done | bytes 131104 | tf_op jit(solution)/shard_map/ppermute | solution.py:441
  142.4 3.4 %collective-permute-done.15.r4 = bf16[2,8,32,128]{3,2,1,0:T(8,128)(2,1)S(1)} collective-permute-done((bf16[2,8,32,128]{3,2,1,0:T(8,128)(2,1)S(1)}, bf16[2,8,32,128]{3,2,1,0:T(8,128)(2,1)S(1)}, u32[]{:S(2)}, u32[]{:S(2)}) %collective-permute-start.15) | collective-permute-done | bytes 131104 | tf_op jit(solution)/shard_map/ppermute | solution.py:441
  145.8 2.7 %shard_map.105 = (f32[512,512]{1,0:T(8,128)S(1)}, bf16[512,512]{1,0:T(8,128)(2,1)S(1)}) custom-call(s32[5]{0:T(128)S(1)} %stack.62.at_ref, bf16[2,512,512]{2,1,0:T(8,128)(2,1)S(1)} %copy-done.1, bf16[2,512,512]{2,1,0:T(8,128)(2,1)S(1)} %copy-done.2, bf16[2,8,32,128]{3,2,1,0:T(8,128)(2,1)S(1)} %pad_maximum_fusion.2.y0, ...), custom_call_target="tpu_custom_call" | custom-call | tf_op jit(solution)/shard_map/pallas_call | solution.py:396
  148.6 3.0 %collective-permute-start.19 = (bf16[512,512]{1,0:T(8,128)(2,1)S(1)}, bf16[512,512]{1,0:T(8,128)(2,1)S(1)}, u32[]{:S(2)}, u32[]{:S(2)}) collective-permute-start(bf16[512,512]{1,0:T(8,128)(2,1)S(1)} %get-tuple-element.28), channel_id=1, source_target_pairs={{0,16},{16,0},{1,17},{17,1},{2,18},{18,2},{3,19},{19,3},{4,20},{20... | collective-permute-start | bytes 1572872 | tf_op jit(solution)/shard_map/ppermute | solution.py:411
  151.6 10.6 %collective-permute-done.19 = bf16[512,512]{1,0:T(8,128)(2,1)S(1)} collective-permute-done((bf16[512,512]{1,0:T(8,128)(2,1)S(1)}, bf16[512,512]{1,0:T(8,128)(2,1)S(1)}, u32[]{:S(2)}, u32[]{:S(2)}) %collective-permute-start.19) | collective-permute-done | bytes 524320 | tf_op jit(solution)/shard_map/ppermute | solution.py:411
  163.1 3.1 %shard_map.107 = (bf16[3,128,512]{2,1,0:T(8,128)(2,1)}, f32[3,3,512]{2,1,0:T(4,128)}, f32[16,512]{1,0:T(8,128)}, f32[16,512]{1,0:T(8,128)}) custom-call(bf16[16,128,128]{2,1,0:T(8,128)(2,1)} %all-to-all-done.3.x_ref), custom_call_target="tpu_custom_call" | custom-call | tf_op jit(solution)/shard_map/pallas_call | solution.py:396
  (44 shorter events, 26.5 us)
Async XLA Ops:
  0.6 18.1 %collective-permute-start = (bf16[128,512]{1,0:T(8,128)(2,1)}, bf16[128,512]{1,0:T(8,128)(2,1)S(1)}, u32[]{:S(2)}, u32[]{:S(2)}) collective-permute-start(bf16[128,512]{1,0:T(8,128)(2,1)} %param.6), channel_id=1, source_target_pairs={{0,0},{2,34},{4,68},{6,102},{8,136},{10,170},{12,204},{14,238},{32... | collective-permute-start | bytes 393224 | tf_op jit(solution)/shard_map/ppermute | solution.py:408
  18.7 19.0 %collective-permute-start.1 = (bf16[128,512]{1,0:T(8,128)(2,1)S(1)}, bf16[128,512]{1,0:T(8,128)(2,1)S(1)}, u32[]{:S(2)}, u32[]{:S(2)}) collective-permute-start(bf16[128,512]{1,0:T(8,128)(2,1)S(1)} %collective-permute-done), channel_id=1, source_target_pairs={{0,8},{8,0},{1,9},{9,1},{2,10},{10,2},{3,11},{11,3},{4,12},{12,4},... | collective-permute-start | bytes 393224 | tf_op jit(solution)/shard_map/ppermute | solution.py:411
  18.7 18.9 %collective-permute-start.3 = (bf16[128,512]{1,0:T(8,128)(2,1)S(1)}, bf16[128,512]{1,0:T(8,128)(2,1)S(1)}, u32[]{:S(2)}, u32[]{:S(2)}) collective-permute-start(bf16[128,512]{1,0:T(8,128)(2,1)S(1)} %collective-permute-done), channel_id=1, source_target_pairs={{0,6},{2,4},{4,2},{6,0},{1,7},{3,5},{5,3},{7,1},{8,14},{10,12},{12... | collective-permute-start | bytes 393224 | tf_op jit(solution)/shard_map/ppermute | solution.py:411
  20.9 16.8 %collective-permute-start.2 = (bf16[128,512]{1,0:T(8,128)(2,1)S(1)}, bf16[128,512]{1,0:T(8,128)(2,1)S(1)}, u32[]{:S(2)}, u32[]{:S(2)}) collective-permute-start(bf16[128,512]{1,0:T(8,128)(2,1)S(1)} %collective-permute-done), channel_id=1, source_target_pairs={{0,2},{2,0},{4,6},{6,4},{1,3},{3,1},{5,7},{7,5},{8,10},{10,8},{12,... | collective-permute-start | bytes 393224 | tf_op jit(solution)/shard_map/ppermute | solution.py:411
  24.9 24.7 %all-to-all-start = ((bf16[16,96,128]{2,1,0:T(8,128)(2,1)}), bf16[16,96,128]{2,1,0:T(8,128)(2,1)S(1)}, u32[]{:S(2)}, u32[]{:S(2)}) async-start(bf16[16,96,128]{2,1,0:T(8,128)(2,1)} %get-tuple-element.20), calls=%async_computation | async-start | bytes 786432 | tf_op jit(solution)/shard_map/all_to_all | solution.py:428
  34.2 18.6 %collective-permute-start.5 = (bf16[512,512]{1,0:T(8,128)(2,1)S(1)}, bf16[512,512]{1,0:T(8,128)(2,1)S(1)}, u32[]{:S(2)}, u32[]{:S(2)}) collective-permute-start(bf16[512,512]{1,0:T(8,128)(2,1)S(1)} %copy-done), channel_id=1, source_target_pairs={{0,16},{16,0},{1,17},{17,1},{2,18},{18,2},{3,19},{19,3},{4,20},{20... | collective-permute-start | bytes 1572872 | tf_op jit(solution)/shard_map/ppermute | solution.py:411
  37.8 15.0 %collective-permute-start.4 = (bf16[4,128,512]{2,1,0:T(8,128)(2,1)S(1)}, bf16[4,128,512]{2,1,0:T(8,128)(2,1)S(1)}, u32[]{:S(2)}, u32[]{:S(2)}) collective-permute-start(bf16[4,128,512]{2,1,0:T(8,128)(2,1)S(1)} %pad_maximum_fusion.mine_ref), channel_id=1, source_target_pairs={{0,1},{1,0},{2,3},{3,2},{4,5},{5,4},{6,7},{7,6},{8,9},{9,8},{10,11... | collective-permute-start | bytes 1572872 | tf_op jit(solution)/shard_map/ppermute | solution.py:411
  55.3 25.7 %all-to-all-start.1 = ((bf16[16,4,32,128]{3,2,1,0:T(8,128)(2,1)}), bf16[16,4,32,128]{3,2,1,0:T(8,128)(2,1)S(1)}, u32[]{:S(2)}, u32[]{:S(2)}) async-start(bf16[16,4,32,128]{3,2,1,0:T(8,128)(2,1)} %get-tuple-element.29), calls=%async_computation.1 | async-start | bytes 1048576 | tf_op jit(solution)/shard_map/all_to_all | solution.py:458
  63.6 6.2 %collective-permute-start.6 = (bf16[128,512]{1,0:T(8,128)(2,1)S(1)}, bf16[128,512]{1,0:T(8,128)(2,1)S(1)}, u32[]{:S(2)}, u32[]{:S(2)}) collective-permute-start(bf16[128,512]{1,0:T(8,128)(2,1)S(1)} %collective-permute-done.1), channel_id=1, source_target_pairs={{0,2},{2,0},{4,6},{6,4},{1,3},{3,1},{5,7},{7,5},{8,10},{10,8},{12,... | collective-permute-start | bytes 393224 | tf_op jit(solution)/shard_map/ppermute | solution.py:411
  64.1 6.9 %collective-permute-start.7 = (bf16[128,512]{1,0:T(8,128)(2,1)S(1)}, bf16[128,512]{1,0:T(8,128)(2,1)S(1)}, u32[]{:S(2)}, u32[]{:S(2)}) collective-permute-start(bf16[128,512]{1,0:T(8,128)(2,1)S(1)} %collective-permute-done.1), channel_id=1, source_target_pairs={{0,6},{2,4},{4,2},{6,0},{1,7},{3,5},{5,3},{7,1},{8,14},{10,12},{12... | collective-permute-start | bytes 393224 | tf_op jit(solution)/shard_map/ppermute | solution.py:411
  66.3 5.3 %collective-permute-start.8 = (bf16[128,512]{1,0:T(8,128)(2,1)S(1)}, bf16[128,512]{1,0:T(8,128)(2,1)S(1)}, u32[]{:S(2)}, u32[]{:S(2)}) collective-permute-start(bf16[128,512]{1,0:T(8,128)(2,1)S(1)} %collective-permute-done.3), channel_id=1, source_target_pairs={{0,2},{2,0},{4,6},{6,4},{1,3},{3,1},{5,7},{7,5},{8,10},{10,8},{12,... | collective-permute-start | bytes 393224 | tf_op jit(solution)/shard_map/ppermute | solution.py:411
  69.8 5.0 %collective-permute-start.9 = (bf16[128,512]{1,0:T(8,128)(2,1)S(1)}, bf16[128,512]{1,0:T(8,128)(2,1)S(1)}, u32[]{:S(2)}, u32[]{:S(2)}) collective-permute-start(bf16[128,512]{1,0:T(8,128)(2,1)S(1)} %collective-permute-done.6), channel_id=1, source_target_pairs={{0,6},{2,4},{4,2},{6,0},{1,7},{3,5},{5,3},{7,1},{8,14},{10,12},{12... | collective-permute-start | bytes 393224 | tf_op jit(solution)/shard_map/ppermute | solution.py:411
  74.9 2.0 %collective-permute-start.10 = (bf16[4,128,512]{2,1,0:T(8,128)(2,1)S(1)}, bf16[4,128,512]{2,1,0:T(8,128)(2,1)S(1)}, u32[]{:S(2)}, u32[]{:S(2)}) collective-permute-start(bf16[4,128,512]{2,1,0:T(8,128)(2,1)S(1)} %pad_maximum_fusion.1.mine_ref), channel_id=1, source_target_pairs={{0,1},{1,0},{2,3},{3,2},{4,5},{5,4},{6,7},{7,6},{8,9},{9,8},{10,11... | collective-permute-start | bytes 1572872 | tf_op jit(solution)/shard_map/ppermute | solution.py:411
  81.0 28.8 %all-to-all-start.2 = ((bf16[16,4,32,128]{3,2,1,0:T(8,128)(2,1)}), bf16[16,4,32,128]{3,2,1,0:T(8,128)(2,1)S(1)}, u32[]{:S(2)}, u32[]{:S(2)}) async-start(bf16[16,4,32,128]{3,2,1,0:T(8,128)(2,1)} %get-tuple-element.30), calls=%async_computation.2 | async-start | bytes 1048576 | tf_op jit(solution)/shard_map/all_to_all | solution.py:458
  88.7 6.2 %collective-permute-start.11 = (bf16[8,32,128]{2,1,0:T(8,128)(2,1)S(1)}, bf16[8,32,128]{2,1,0:T(8,128)(2,1)S(1)}, u32[]{:S(2)}, u32[]{:S(2)}) collective-permute-start(bf16[8,32,128]{2,1,0:T(8,128)(2,1)S(1)} %get-tuple-element.26), channel_id=1, source_target_pairs={{0,16},{16,0},{1,17},{17,1},{2,18},{18,2},{3,19},{19,3},{4,20},{20... | collective-permute-start | bytes 196616 | tf_op jit(solution)/shard_map/ppermute | solution.py:411
  94.9 11.6 %collective-permute-start.12 = (bf16[2,8,32,128]{3,2,1,0:T(8,128)(2,1)S(1)}, bf16[2,8,32,128]{3,2,1,0:T(8,128)(2,1)S(1)}, u32[]{:S(2)}, u32[]{:S(2)}) collective-permute-start(bf16[2,8,32,128]{3,2,1,0:T(8,128)(2,1)S(1)} %pad_maximum_fusion.2.y0), channel_id=1, source_target_pairs={{0,32},{32,64},{64,96},{96,128},{128,160},{160,192},{192,224},{224... | collective-permute-start | bytes 393224 | tf_op jit(solution)/shard_map/ppermute | solution.py:441
  96.8 9.7 %collective-permute-start.16 = (bf16[2,8,32,128]{3,2,1,0:T(8,128)(2,1)S(1)}, bf16[2,8,32,128]{3,2,1,0:T(8,128)(2,1)S(1)}, u32[]{:S(2)}, u32[]{:S(2)}) collective-permute-start(bf16[2,8,32,128]{3,2,1,0:T(8,128)(2,1)S(1)} %pad_maximum_fusion.2.y0), channel_id=1, source_target_pairs={{0,224},{32,0},{64,32},{96,64},{128,96},{160,128},{192,160},{224,1... | collective-permute-start | bytes 393224 | tf_op jit(solution)/shard_map/ppermute | solution.py:441
  106.5 17.1 %collective-permute-start.13 = (bf16[2,8,32,128]{3,2,1,0:T(8,128)(2,1)S(1)}, bf16[2,8,32,128]{3,2,1,0:T(8,128)(2,1)S(1)}, u32[]{:S(2)}, u32[]{:S(2)}) collective-permute-start(bf16[2,8,32,128]{3,2,1,0:T(8,128)(2,1)S(1)} %collective-permute-done.12.r1), channel_id=1, source_target_pairs={{0,32},{32,64},{64,96},{96,128},{128,160},{160,192},{192,224},{224... | collective-permute-start | bytes 393224 | tf_op jit(solution)/shard_map/ppermute | solution.py:441
  106.5 21.5 %collective-permute-start.17 = (bf16[2,8,32,128]{3,2,1,0:T(8,128)(2,1)S(1)}, bf16[2,8,32,128]{3,2,1,0:T(8,128)(2,1)S(1)}, u32[]{:S(2)}, u32[]{:S(2)}) collective-permute-start(bf16[2,8,32,128]{3,2,1,0:T(8,128)(2,1)S(1)} %collective-permute-done.16.l1), channel_id=1, source_target_pairs={{0,224},{32,0},{64,32},{96,64},{128,96},{160,128},{192,160},{224,1... | collective-permute-start | bytes 393224 | tf_op jit(solution)/shard_map/ppermute | solution.py:441
  116.4 46.7 %all-to-all-start.3 = ((bf16[16,128,128]{2,1,0:T(8,128)(2,1)}), bf16[16,128,128]{2,1,0:T(8,128)(2,1)}, u32[]{:S(2)}, u32[]{:S(2)}) async-start(bf16[16,128,128]{2,1,0:T(8,128)(2,1)} %shard_map.106), calls=%async_computation.3 | async-start | bytes 1048576 | tf_op jit(solution)/shard_map/all_to_all | solution.py:472
  123.7 18.7 %collective-permute-start.14 = (bf16[2,8,32,128]{3,2,1,0:T(8,128)(2,1)S(1)}, bf16[2,8,32,128]{3,2,1,0:T(8,128)(2,1)S(1)}, u32[]{:S(2)}, u32[]{:S(2)}) collective-permute-start(bf16[2,8,32,128]{3,2,1,0:T(8,128)(2,1)S(1)} %collective-permute-done.13.r2), channel_id=1, source_target_pairs={{0,32},{32,64},{64,96},{96,128},{128,160},{160,192},{192,224},{224... | collective-permute-start | bytes 393224 | tf_op jit(solution)/shard_map/ppermute | solution.py:441
  125.6 20.2 %collective-permute-start.15 = (bf16[2,8,32,128]{3,2,1,0:T(8,128)(2,1)S(1)}, bf16[2,8,32,128]{3,2,1,0:T(8,128)(2,1)S(1)}, u32[]{:S(2)}, u32[]{:S(2)}) collective-permute-start(bf16[2,8,32,128]{3,2,1,0:T(8,128)(2,1)S(1)} %collective-permute-done.13.r2), channel_id=1, source_target_pairs={{0,64},{32,96},{64,128},{96,160},{128,192},{160,224},{192,0},{224,... | collective-permute-start | bytes 393224 | tf_op jit(solution)/shard_map/ppermute | solution.py:441
  128.0 17.8 %collective-permute-start.18 = (bf16[2,8,32,128]{3,2,1,0:T(8,128)(2,1)S(1)}, bf16[2,8,32,128]{3,2,1,0:T(8,128)(2,1)S(1)}, u32[]{:S(2)}, u32[]{:S(2)}) collective-permute-start(bf16[2,8,32,128]{3,2,1,0:T(8,128)(2,1)S(1)} %collective-permute-done.17.l2), channel_id=1, source_target_pairs={{0,224},{32,0},{64,32},{96,64},{128,96},{160,128},{192,160},{224,1... | collective-permute-start | bytes 393224 | tf_op jit(solution)/shard_map/ppermute | solution.py:441
  148.6 13.6 %collective-permute-start.19 = (bf16[512,512]{1,0:T(8,128)(2,1)S(1)}, bf16[512,512]{1,0:T(8,128)(2,1)S(1)}, u32[]{:S(2)}, u32[]{:S(2)}) collective-permute-start(bf16[512,512]{1,0:T(8,128)(2,1)S(1)} %get-tuple-element.28), channel_id=1, source_target_pairs={{0,16},{16,0},{1,17},{17,1},{2,18},{18,2},{3,19},{19,3},{4,20},{20... | collective-permute-start | bytes 1572872 | tf_op jit(solution)/shard_map/ppermute | solution.py:411
  (4 other events, 88.9 us)

commit v4 on v3

--- a/solution.py
+++ b/solution.py
@@ -113,7 +113,7 @@
             return tuple(decay8[n] * state[n] + value for n in range(NM))
 
         state = lax.fori_loop(
-            0, STEPS, step, tuple(jnp.zeros((8, 128), F32) for _ in range(NM)), unroll=4
+            0, STEPS, step, tuple(jnp.zeros((8, 128), F32) for _ in range(NM)), unroll=8
         )
         for n in range(NM):
             out[n * NK + v * 8 : n * NK + v * 8 + 8, :] = state[n]
@@ -164,7 +164,7 @@
             STEPS,
             step,
             tuple(in_ref[n * NK + v * 8 : n * NK + v * 8 + 8, :] for n in range(NM)),
-            unroll=2,
+            unroll=4,
         )
     h = at_ref[1]
     for k in range(8):
@@ -225,7 +225,7 @@
             STEPS,
             forward,
             tuple(in_ref[n * NK + v * 8 : n * NK + v * 8 + 8, :] for n in range(NM)),
-            unroll=2,
+            unroll=4,
         )
     spot = at_ref[3]
     wide[0:ROWS, :] = jnp.zeros((ROWS, 128), F32)
@@ -270,7 +270,7 @@
 
             zeros = tuple(zero for _ in range(8))
             first = tuple(tails[n * NK + v * 8 : n * NK + v * 8 + 8, :] for n in modes)
-            _, by_res, by_rate = lax.fori_loop(0, STEPS, backward, (first, zeros, zeros), unroll=2)
+            _, by_res, by_rate = lax.fori_loop(0, STEPS, backward, (first, zeros, zeros), unroll=4)
             for m, n in enumerate(modes):
                 rate_part = by_rate[m] * (-decay[m] * weight[m])
                 to_res = pl.ds((RES + n) * 8, 8)

time: 169 us -> 169 us (level)
  no operation moved by 1% of the time
where the time goes in v4:
time: 169 us; the launch traced here: 166 us
  waiting for transfers between devices  71.2 us (42%)
  starting transfers between devices  70.6 us (42%)
  Pallas kernels  22.1 us (13%)
    ppermute x7, waiting for transfers between devices, turn(): return lax.ppermute(value, 'z', [(i, (i + by) % 8) for i in range(8)])  24.3 us
    pallas_call x7, Pallas kernels, run(): return pl.pallas_call(kernel, **settings)(*args)  22.1 us
    ppermute x12, waiting for transfers between devices, flip(): lax.ppermute(value, axis, [(i, i ^ by) for i in range(lax.axis_size(axis))])  20.7 us
    ppermute x12, starting transfers between devices, flip(): lax.ppermute(value, axis, [(i, i ^ by) for i in range(lax.axis_size(axis))])  20.4 us
    all_to_all x2, starting transfers between devices, compute(): grads.append(lax.all_to_all(parts, CTX, 0, 0))  16 us
    ppermute x1, waiting for transfers between devices, compute(): moved = lax.ppermute(out_grad, ('z', 'xl', 'y'), route)  12.9 us
    ppermute x7, starting transfers between devices, turn(): return lax.ppermute(value, 'z', [(i, (i + by) % 8) for i in range(8)])  12.6 us
    all_to_all x1, waiting for transfers between devices, compute(): x = lax.all_to_all(chunks, CTX, 0, 0)  11.7 us
  transfers between devices with their start and end apart: 24, of which 13 were waited for; matrix products, arithmetic and copies ran while one was open for 1% of the time, Pallas kernels for 10%

profile of v4, /device:TPU:16, one launch (start us, length us, event | category | flops | bytes accessed | tf_op | source)
XLA Modules:
  0.0 165.9 jit_solution(12455129628626192645)
XLA Ops:
  0.6 5.2 %collective-permute-start = (bf16[128,512]{1,0:T(8,128)(2,1)}, bf16[128,512]{1,0:T(8,128)(2,1)S(1)}, u32[]{:S(2)}, u32[]{:S(2)}) collective-permute-start(bf16[128,512]{1,0:T(8,128)(2,1)} %param.6), channel_id=1, source_target_pairs={{0,0},{2,34},{4,68},{6,102},{8,136},{10,170},{12,204},{14,238},{32... | collective-permute-start | bytes 393224 | tf_op jit(solution)/shard_map/ppermute | solution.py:408
  5.8 12.9 %collective-permute-done = bf16[128,512]{1,0:T(8,128)(2,1)S(1)} collective-permute-done((bf16[128,512]{1,0:T(8,128)(2,1)}, bf16[128,512]{1,0:T(8,128)(2,1)S(1)}, u32[]{:S(2)}, u32[]{:S(2)}) %collective-permute-start) | collective-permute-done | bytes 131104 | tf_op jit(solution)/shard_map/ppermute | solution.py:408
  24.9 9.2 %all-to-all-start = ((bf16[16,96,128]{2,1,0:T(8,128)(2,1)}), bf16[16,96,128]{2,1,0:T(8,128)(2,1)S(1)}, u32[]{:S(2)}, u32[]{:S(2)}) async-start(bf16[16,96,128]{2,1,0:T(8,128)(2,1)} %get-tuple-element.20), calls=%async_computation | async-start | bytes 786432 | tf_op jit(solution)/shard_map/all_to_all | solution.py:428
  34.2 3.5 %collective-permute-start.5 = (bf16[512,512]{1,0:T(8,128)(2,1)S(1)}, bf16[512,512]{1,0:T(8,128)(2,1)S(1)}, u32[]{:S(2)}, u32[]{:S(2)}) collective-permute-start(bf16[512,512]{1,0:T(8,128)(2,1)S(1)} %copy-done), channel_id=1, source_target_pairs={{0,16},{16,0},{1,17},{17,1},{2,18},{18,2},{3,19},{19,3},{4,20},{20... | collective-permute-start | bytes 1572872 | tf_op jit(solution)/shard_map/ppermute | solution.py:411
  38.0 11.7 %all-to-all-done.x_ref = bf16[16,96,128]{2,1,0:T(8,128)(2,1)S(1)} async-done(((bf16[16,96,128]{2,1,0:T(8,128)(2,1)}), bf16[16,96,128]{2,1,0:T(8,128)(2,1)S(1)}, u32[]{:S(2)}, u32[]{:S(2)}) %all-to-all-start) | async-done | bytes 393248 | tf_op jit(solution)/shard_map/all_to_all | solution.py:428
  49.7 2.7 %shard_map.102 = (bf16[8,32,128]{2,1,0:T(8,128)(2,1)S(1)}, bf16[8,32,128]{2,1,0:T(8,128)(2,1)S(1)}, f32[256,128]{1,0:T(8,128)S(1)}) custom-call(s32[5]{0:T(128)S(1)} %stack.62.at_ref, bf16[16,96,128]{2,1,0:T(8,128)(2,1)S(1)} %all-to-all-done.x_ref, f32[56,128]{1,0:T(8,128)S(1)} %copy-done.3), custom_call_target="tpu_custom_call" | custom-call | tf_op jit(solution)/shard_map/pallas_call | solution.py:396
  52.8 2.5 %shard_map.103 = (bf16[16,4,32,128]{3,2,1,0:T(8,128)(2,1)}, bf16[2,512,512]{2,1,0:T(8,128)(2,1)}) custom-call(s32[5]{0:T(128)S(1)} %stack.62.at_ref, bf16[4,128,512]{2,1,0:T(8,128)(2,1)S(1)} %pad_maximum_fusion.mine_ref, bf16[4,128,512]{2,1,0:T(8,128)(2,1)S(1)} %collective-permute-done.4.theirs_ref, bf16[512,512]{1,0:T(8,128)(2,1)S(1)} %copy-done, ...), custom_call_target="tpu_custom_call" | custom-call | tf_op jit(solution)/shard_map/pallas_call | solution.py:396
  55.3 8.3 %all-to-all-start.1 = ((bf16[16,4,32,128]{3,2,1,0:T(8,128)(2,1)}), bf16[16,4,32,128]{3,2,1,0:T(8,128)(2,1)S(1)}, u32[]{:S(2)}, u32[]{:S(2)}) async-start(bf16[16,4,32,128]{3,2,1,0:T(8,128)(2,1)} %get-tuple-element.29), calls=%async_computation.1 | async-start | bytes 1048576 | tf_op jit(solution)/shard_map/all_to_all | solution.py:458
  71.6 3.2 %collective-permute-done.9 = bf16[128,512]{1,0:T(8,128)(2,1)S(1)} collective-permute-done((bf16[128,512]{1,0:T(8,128)(2,1)S(1)}, bf16[128,512]{1,0:T(8,128)(2,1)S(1)}, u32[]{:S(2)}, u32[]{:S(2)}) %collective-permute-start.9) | collective-permute-done | bytes 131104 | tf_op jit(solution)/shard_map/ppermute | solution.py:411
  76.8 2.6 %shard_map.104 = (bf16[16,4,32,128]{3,2,1,0:T(8,128)(2,1)}, bf16[2,512,512]{2,1,0:T(8,128)(2,1)}) custom-call(s32[5]{0:T(128)S(1)} %stack.62.at_ref, bf16[4,128,512]{2,1,0:T(8,128)(2,1)S(1)} %pad_maximum_fusion.1.mine_ref, bf16[4,128,512]{2,1,0:T(8,128)(2,1)S(1)} %collective-permute-done.10.theirs_ref, bf16[512,512]{1,0:T(8,128)(2,1)S(1)} %copy-done, ...), custom_call_target="tpu_custom_call" | custom-call | tf_op jit(solution)/shard_map/pallas_call | solution.py:396
  81.0 7.7 %all-to-all-start.2 = ((bf16[16,4,32,128]{3,2,1,0:T(8,128)(2,1)}), bf16[16,4,32,128]{3,2,1,0:T(8,128)(2,1)S(1)}, u32[]{:S(2)}, u32[]{:S(2)}) async-start(bf16[16,4,32,128]{3,2,1,0:T(8,128)(2,1)} %get-tuple-element.30), calls=%async_computation.2 | async-start | bytes 1048576 | tf_op jit(solution)/shard_map/all_to_all | solution.py:458
  88.7 3.4 %collective-permute-start.11 = (bf16[8,32,128]{2,1,0:T(8,128)(2,1)S(1)}, bf16[8,32,128]{2,1,0:T(8,128)(2,1)S(1)}, u32[]{:S(2)}, u32[]{:S(2)}) collective-permute-start(bf16[8,32,128]{2,1,0:T(8,128)(2,1)S(1)} %get-tuple-element.26), channel_id=1, source_target_pairs={{0,16},{16,0},{1,17},{17,1},{2,18},{18,2},{3,19},{19,3},{4,20},{20... | collective-permute-start | bytes 196616 | tf_op jit(solution)/shard_map/ppermute | solution.py:411
  92.1 2.8 %collective-permute-done.11 = bf16[8,32,128]{2,1,0:T(8,128)(2,1)S(1)} collective-permute-done((bf16[8,32,128]{2,1,0:T(8,128)(2,1)S(1)}, bf16[8,32,128]{2,1,0:T(8,128)(2,1)S(1)}, u32[]{:S(2)}, u32[]{:S(2)}) %collective-permute-start.11) | collective-permute-done | bytes 65568 | tf_op jit(solution)/shard_map/ppermute | solution.py:411
  98.3 8.3 %collective-permute-done.12.r1 = bf16[2,8,32,128]{3,2,1,0:T(8,128)(2,1)S(1)} collective-permute-done((bf16[2,8,32,128]{3,2,1,0:T(8,128)(2,1)S(1)}, bf16[2,8,32,128]{3,2,1,0:T(8,128)(2,1)S(1)}, u32[]{:S(2)}, u32[]{:S(2)}) %collective-permute-start.12) | collective-permute-done | bytes 131104 | tf_op jit(solution)/shard_map/ppermute | solution.py:441
  106.5 3.2 %collective-permute-start.17 = (bf16[2,8,32,128]{3,2,1,0:T(8,128)(2,1)S(1)}, bf16[2,8,32,128]{3,2,1,0:T(8,128)(2,1)S(1)}, u32[]{:S(2)}, u32[]{:S(2)}) collective-permute-start(bf16[2,8,32,128]{3,2,1,0:T(8,128)(2,1)S(1)} %collective-permute-done.16.l1), channel_id=1, source_target_pairs={{0,224},{32,0},{64,32},{96,64},{128,96},{160,128},{192,160},{224,1... | collective-permute-start | bytes 393224 | tf_op jit(solution)/shard_map/ppermute | solution.py:441
  109.8 6.3 %shard_map.106 = bf16[16,128,128]{2,1,0:T(8,128)(2,1)} custom-call(s32[5]{0:T(128)S(1)} %stack.62.at_ref, bf16[16,96,128]{2,1,0:T(8,128)(2,1)S(1)} %all-to-all-done.x_ref, f32[56,128]{1,0:T(8,128)S(1)} %copy-done.3, f32[256,128]{1,0:T(8,128)S(1)} %get-tuple-element.22.after_ref.in_ref, bf16[16,4,32,128]{3,2,1,0:T(8,128)(2,1)S(1)} %all-to-all-done.1.gy1_ref, ...), custom_call_target="tpu_custom_call" | custom-call | tf_op jit(solution)/shard_map/pallas_call | solution.py:396
  116.0 7.2 %all-to-all-start.3 = ((bf16[16,128,128]{2,1,0:T(8,128)(2,1)}), bf16[16,128,128]{2,1,0:T(8,128)(2,1)}, u32[]{:S(2)}, u32[]{:S(2)}) async-start(bf16[16,128,128]{2,1,0:T(8,128)(2,1)} %shard_map.106), calls=%async_computation.3 | async-start | bytes 1048576 | tf_op jit(solution)/shard_map/all_to_all | solution.py:472
  125.2 2.4 %collective-permute-start.15 = (bf16[2,8,32,128]{3,2,1,0:T(8,128)(2,1)S(1)}, bf16[2,8,32,128]{3,2,1,0:T(8,128)(2,1)S(1)}, u32[]{:S(2)}, u32[]{:S(2)}) collective-permute-start(bf16[2,8,32,128]{3,2,1,0:T(8,128)(2,1)S(1)} %collective-permute-done.13.r2), channel_id=1, source_target_pairs={{0,64},{32,96},{64,128},{96,160},{128,192},{160,224},{192,0},{224,... | collective-permute-start | bytes 393224 | tf_op jit(solution)/shard_map/ppermute | solution.py:441
  129.3 12.7 %collective-permute-done.14.r3 = bf16[2,8,32,128]{3,2,1,0:T(8,128)(2,1)S(1)} collective-permute-done((bf16[2,8,32,128]{3,2,1,0:T(8,128)(2,1)S(1)}, bf16[2,8,32,128]{3,2,1,0:T(8,128)(2,1)S(1)}, u32[]{:S(2)}, u32[]{:S(2)}) %collective-permute-start.14) | collective-permute-done | bytes 131104 | tf_op jit(solution)/shard_map/ppermute | solution.py:441
  142.0 3.4 %collective-permute-done.15.r4 = bf16[2,8,32,128]{3,2,1,0:T(8,128)(2,1)S(1)} collective-permute-done((bf16[2,8,32,128]{3,2,1,0:T(8,128)(2,1)S(1)}, bf16[2,8,32,128]{3,2,1,0:T(8,128)(2,1)S(1)}, u32[]{:S(2)}, u32[]{:S(2)}) %collective-permute-start.15) | collective-permute-done | bytes 131104 | tf_op jit(solution)/shard_map/ppermute | solution.py:441
  145.4 2.7 %shard_map.105 = (f32[512,512]{1,0:T(8,128)S(1)}, bf16[512,512]{1,0:T(8,128)(2,1)S(1)}) custom-call(s32[5]{0:T(128)S(1)} %stack.62.at_ref, bf16[2,512,512]{2,1,0:T(8,128)(2,1)S(1)} %copy-done.1, bf16[2,512,512]{2,1,0:T(8,128)(2,1)S(1)} %copy-done.2, bf16[2,8,32,128]{3,2,1,0:T(8,128)(2,1)S(1)} %pad_maximum_fusion.2.y0, ...), custom_call_target="tpu_custom_call" | custom-call | tf_op jit(solution)/shard_map/pallas_call | solution.py:396
  148.1 3.1 %collective-permute-start.19 = (bf16[512,512]{1,0:T(8,128)(2,1)S(1)}, bf16[512,512]{1,0:T(8,128)(2,1)S(1)}, u32[]{:S(2)}, u32[]{:S(2)}) collective-permute-start(bf16[512,512]{1,0:T(8,128)(2,1)S(1)} %get-tuple-element.28), channel_id=1, source_target_pairs={{0,16},{16,0},{1,17},{17,1},{2,18},{18,2},{3,19},{19,3},{4,20},{20... | collective-permute-start | bytes 1572872 | tf_op jit(solution)/shard_map/ppermute | solution.py:411
  151.2 10.6 %collective-permute-done.19 = bf16[512,512]{1,0:T(8,128)(2,1)S(1)} collective-permute-done((bf16[512,512]{1,0:T(8,128)(2,1)S(1)}, bf16[512,512]{1,0:T(8,128)(2,1)S(1)}, u32[]{:S(2)}, u32[]{:S(2)}) %collective-permute-start.19) | collective-permute-done | bytes 524320 | tf_op jit(solution)/shard_map/ppermute | solution.py:411
  162.7 3.1 %shard_map.107 = (bf16[3,128,512]{2,1,0:T(8,128)(2,1)}, f32[3,3,512]{2,1,0:T(4,128)}, f32[16,512]{1,0:T(8,128)}, f32[16,512]{1,0:T(8,128)}) custom-call(bf16[16,128,128]{2,1,0:T(8,128)(2,1)} %all-to-all-done.3.x_ref), custom_call_target="tpu_custom_call" | custom-call | tf_op jit(solution)/shard_map/pallas_call | solution.py:396
  (44 shorter events, 26.6 us)
Async XLA Ops:
  0.6 18.1 %collective-permute-start = (bf16[128,512]{1,0:T(8,128)(2,1)}, bf16[128,512]{1,0:T(8,128)(2,1)S(1)}, u32[]{:S(2)}, u32[]{:S(2)}) collective-permute-start(bf16[128,512]{1,0:T(8,128)(2,1)} %param.6), channel_id=1, source_target_pairs={{0,0},{2,34},{4,68},{6,102},{8,136},{10,170},{12,204},{14,238},{32... | collective-permute-start | bytes 393224 | tf_op jit(solution)/shard_map/ppermute | solution.py:408
  18.7 19.0 %collective-permute-start.1 = (bf16[128,512]{1,0:T(8,128)(2,1)S(1)}, bf16[128,512]{1,0:T(8,128)(2,1)S(1)}, u32[]{:S(2)}, u32[]{:S(2)}) collective-permute-start(bf16[128,512]{1,0:T(8,128)(2,1)S(1)} %collective-permute-done), channel_id=1, source_target_pairs={{0,8},{8,0},{1,9},{9,1},{2,10},{10,2},{3,11},{11,3},{4,12},{12,4},... | collective-permute-start | bytes 393224 | tf_op jit(solution)/shard_map/ppermute | solution.py:411
  18.7 18.9 %collective-permute-start.3 = (bf16[128,512]{1,0:T(8,128)(2,1)S(1)}, bf16[128,512]{1,0:T(8,128)(2,1)S(1)}, u32[]{:S(2)}, u32[]{:S(2)}) collective-permute-start(bf16[128,512]{1,0:T(8,128)(2,1)S(1)} %collective-permute-done), channel_id=1, source_target_pairs={{0,6},{2,4},{4,2},{6,0},{1,7},{3,5},{5,3},{7,1},{8,14},{10,12},{12... | collective-permute-start | bytes 393224 | tf_op jit(solution)/shard_map/ppermute | solution.py:411
  20.9 16.8 %collective-permute-start.2 = (bf16[128,512]{1,0:T(8,128)(2,1)S(1)}, bf16[128,512]{1,0:T(8,128)(2,1)S(1)}, u32[]{:S(2)}, u32[]{:S(2)}) collective-permute-start(bf16[128,512]{1,0:T(8,128)(2,1)S(1)} %collective-permute-done), channel_id=1, source_target_pairs={{0,2},{2,0},{4,6},{6,4},{1,3},{3,1},{5,7},{7,5},{8,10},{10,8},{12,... | collective-permute-start | bytes 393224 | tf_op jit(solution)/shard_map/ppermute | solution.py:411
  24.9 24.7 %all-to-all-start = ((bf16[16,96,128]{2,1,0:T(8,128)(2,1)}), bf16[16,96,128]{2,1,0:T(8,128)(2,1)S(1)}, u32[]{:S(2)}, u32[]{:S(2)}) async-start(bf16[16,96,128]{2,1,0:T(8,128)(2,1)} %get-tuple-element.20), calls=%async_computation | async-start | bytes 786432 | tf_op jit(solution)/shard_map/all_to_all | solution.py:428
  34.2 18.6 %collective-permute-start.5 = (bf16[512,512]{1,0:T(8,128)(2,1)S(1)}, bf16[512,512]{1,0:T(8,128)(2,1)S(1)}, u32[]{:S(2)}, u32[]{:S(2)}) collective-permute-start(bf16[512,512]{1,0:T(8,128)(2,1)S(1)} %copy-done), channel_id=1, source_target_pairs={{0,16},{16,0},{1,17},{17,1},{2,18},{18,2},{3,19},{19,3},{4,20},{20... | collective-permute-start | bytes 1572872 | tf_op jit(solution)/shard_map/ppermute | solution.py:411
  37.8 15.0 %collective-permute-start.4 = (bf16[4,128,512]{2,1,0:T(8,128)(2,1)S(1)}, bf16[4,128,512]{2,1,0:T(8,128)(2,1)S(1)}, u32[]{:S(2)}, u32[]{:S(2)}) collective-permute-start(bf16[4,128,512]{2,1,0:T(8,128)(2,1)S(1)} %pad_maximum_fusion.mine_ref), channel_id=1, source_target_pairs={{0,1},{1,0},{2,3},{3,2},{4,5},{5,4},{6,7},{7,6},{8,9},{9,8},{10,11... | collective-permute-start | bytes 1572872 | tf_op jit(solution)/shard_map/ppermute | solution.py:411
  55.3 25.7 %all-to-all-start.1 = ((bf16[16,4,32,128]{3,2,1,0:T(8,128)(2,1)}), bf16[16,4,32,128]{3,2,1,0:T(8,128)(2,1)S(1)}, u32[]{:S(2)}, u32[]{:S(2)}) async-start(bf16[16,4,32,128]{3,2,1,0:T(8,128)(2,1)} %get-tuple-element.29), calls=%async_computation.1 | async-start | bytes 1048576 | tf_op jit(solution)/shard_map/all_to_all | solution.py:458
  63.6 6.2 %collective-permute-start.6 = (bf16[128,512]{1,0:T(8,128)(2,1)S(1)}, bf16[128,512]{1,0:T(8,128)(2,1)S(1)}, u32[]{:S(2)}, u32[]{:S(2)}) collective-permute-start(bf16[128,512]{1,0:T(8,128)(2,1)S(1)} %collective-permute-done.1), channel_id=1, source_target_pairs={{0,2},{2,0},{4,6},{6,4},{1,3},{3,1},{5,7},{7,5},{8,10},{10,8},{12,... | collective-permute-start | bytes 393224 | tf_op jit(solution)/shard_map/ppermute | solution.py:411
  64.1 6.9 %collective-permute-start.7 = (bf16[128,512]{1,0:T(8,128)(2,1)S(1)}, bf16[128,512]{1,0:T(8,128)(2,1)S(1)}, u32[]{:S(2)}, u32[]{:S(2)}) collective-permute-start(bf16[128,512]{1,0:T(8,128)(2,1)S(1)} %collective-permute-done.1), channel_id=1, source_target_pairs={{0,6},{2,4},{4,2},{6,0},{1,7},{3,5},{5,3},{7,1},{8,14},{10,12},{12... | collective-permute-start | bytes 393224 | tf_op jit(solution)/shard_map/ppermute | solution.py:411
  66.3 5.3 %collective-permute-start.8 = (bf16[128,512]{1,0:T(8,128)(2,1)S(1)}, bf16[128,512]{1,0:T(8,128)(2,1)S(1)}, u32[]{:S(2)}, u32[]{:S(2)}) collective-permute-start(bf16[128,512]{1,0:T(8,128)(2,1)S(1)} %collective-permute-done.3), channel_id=1, source_target_pairs={{0,2},{2,0},{4,6},{6,4},{1,3},{3,1},{5,7},{7,5},{8,10},{10,8},{12,... | collective-permute-start | bytes 393224 | tf_op jit(solution)/shard_map/ppermute | solution.py:411
  69.8 5.0 %collective-permute-start.9 = (bf16[128,512]{1,0:T(8,128)(2,1)S(1)}, bf16[128,512]{1,0:T(8,128)(2,1)S(1)}, u32[]{:S(2)}, u32[]{:S(2)}) collective-permute-start(bf16[128,512]{1,0:T(8,128)(2,1)S(1)} %collective-permute-done.6), channel_id=1, source_target_pairs={{0,6},{2,4},{4,2},{6,0},{1,7},{3,5},{5,3},{7,1},{8,14},{10,12},{12... | collective-permute-start | bytes 393224 | tf_op jit(solution)/shard_map/ppermute | solution.py:411
  74.9 2.0 %collective-permute-start.10 = (bf16[4,128,512]{2,1,0:T(8,128)(2,1)S(1)}, bf16[4,128,512]{2,1,0:T(8,128)(2,1)S(1)}, u32[]{:S(2)}, u32[]{:S(2)}) collective-permute-start(bf16[4,128,512]{2,1,0:T(8,128)(2,1)S(1)} %pad_maximum_fusion.1.mine_ref), channel_id=1, source_target_pairs={{0,1},{1,0},{2,3},{3,2},{4,5},{5,4},{6,7},{7,6},{8,9},{9,8},{10,11... | collective-permute-start | bytes 1572872 | tf_op jit(solution)/shard_map/ppermute | solution.py:411
  81.0 28.8 %all-to-all-start.2 = ((bf16[16,4,32,128]{3,2,1,0:T(8,128)(2,1)}), bf16[16,4,32,128]{3,2,1,0:T(8,128)(2,1)S(1)}, u32[]{:S(2)}, u32[]{:S(2)}) async-start(bf16[16,4,32,128]{3,2,1,0:T(8,128)(2,1)} %get-tuple-element.30), calls=%async_computation.2 | async-start | bytes 1048576 | tf_op jit(solution)/shard_map/all_to_all | solution.py:458
  88.7 6.2 %collective-permute-start.11 = (bf16[8,32,128]{2,1,0:T(8,128)(2,1)S(1)}, bf16[8,32,128]{2,1,0:T(8,128)(2,1)S(1)}, u32[]{:S(2)}, u32[]{:S(2)}) collective-permute-start(bf16[8,32,128]{2,1,0:T(8,128)(2,1)S(1)} %get-tuple-element.26), channel_id=1, source_target_pairs={{0,16},{16,0},{1,17},{17,1},{2,18},{18,2},{3,19},{19,3},{4,20},{20... | collective-permute-start | bytes 196616 | tf_op jit(solution)/shard_map/ppermute | solution.py:411
  94.9 11.6 %collective-permute-start.12 = (bf16[2,8,32,128]{3,2,1,0:T(8,128)(2,1)S(1)}, bf16[2,8,32,128]{3,2,1,0:T(8,128)(2,1)S(1)}, u32[]{:S(2)}, u32[]{:S(2)}) collective-permute-start(bf16[2,8,32,128]{3,2,1,0:T(8,128)(2,1)S(1)} %pad_maximum_fusion.2.y0), channel_id=1, source_target_pairs={{0,32},{32,64},{64,96},{96,128},{128,160},{160,192},{192,224},{224... | collective-permute-start | bytes 393224 | tf_op jit(solution)/shard_map/ppermute | solution.py:441
  96.8 9.7 %collective-permute-start.16 = (bf16[2,8,32,128]{3,2,1,0:T(8,128)(2,1)S(1)}, bf16[2,8,32,128]{3,2,1,0:T(8,128)(2,1)S(1)}, u32[]{:S(2)}, u32[]{:S(2)}) collective-permute-start(bf16[2,8,32,128]{3,2,1,0:T(8,128)(2,1)S(1)} %pad_maximum_fusion.2.y0), channel_id=1, source_target_pairs={{0,224},{32,0},{64,32},{96,64},{128,96},{160,128},{192,160},{224,1... | collective-permute-start | bytes 393224 | tf_op jit(solution)/shard_map/ppermute | solution.py:441
  106.5 16.7 %collective-permute-start.13 = (bf16[2,8,32,128]{3,2,1,0:T(8,128)(2,1)S(1)}, bf16[2,8,32,128]{3,2,1,0:T(8,128)(2,1)S(1)}, u32[]{:S(2)}, u32[]{:S(2)}) collective-permute-start(bf16[2,8,32,128]{3,2,1,0:T(8,128)(2,1)S(1)} %collective-permute-done.12.r1), channel_id=1, source_target_pairs={{0,32},{32,64},{64,96},{96,128},{128,160},{160,192},{192,224},{224... | collective-permute-start | bytes 393224 | tf_op jit(solution)/shard_map/ppermute | solution.py:441
  106.5 21.0 %collective-permute-start.17 = (bf16[2,8,32,128]{3,2,1,0:T(8,128)(2,1)S(1)}, bf16[2,8,32,128]{3,2,1,0:T(8,128)(2,1)S(1)}, u32[]{:S(2)}, u32[]{:S(2)}) collective-permute-start(bf16[2,8,32,128]{3,2,1,0:T(8,128)(2,1)S(1)} %collective-permute-done.16.l1), channel_id=1, source_target_pairs={{0,224},{32,0},{64,32},{96,64},{128,96},{160,128},{192,160},{224,1... | collective-permute-start | bytes 393224 | tf_op jit(solution)/shard_map/ppermute | solution.py:441
  116.0 46.7 %all-to-all-start.3 = ((bf16[16,128,128]{2,1,0:T(8,128)(2,1)}), bf16[16,128,128]{2,1,0:T(8,128)(2,1)}, u32[]{:S(2)}, u32[]{:S(2)}) async-start(bf16[16,128,128]{2,1,0:T(8,128)(2,1)} %shard_map.106), calls=%async_computation.3 | async-start | bytes 1048576 | tf_op jit(solution)/shard_map/all_to_all | solution.py:472
  123.2 18.7 %collective-permute-start.14 = (bf16[2,8,32,128]{3,2,1,0:T(8,128)(2,1)S(1)}, bf16[2,8,32,128]{3,2,1,0:T(8,128)(2,1)S(1)}, u32[]{:S(2)}, u32[]{:S(2)}) collective-permute-start(bf16[2,8,32,128]{3,2,1,0:T(8,128)(2,1)S(1)} %collective-permute-done.13.r2), channel_id=1, source_target_pairs={{0,32},{32,64},{64,96},{96,128},{128,160},{160,192},{192,224},{224... | collective-permute-start | bytes 393224 | tf_op jit(solution)/shard_map/ppermute | solution.py:441
  125.2 20.2 %collective-permute-start.15 = (bf16[2,8,32,128]{3,2,1,0:T(8,128)(2,1)S(1)}, bf16[2,8,32,128]{3,2,1,0:T(8,128)(2,1)S(1)}, u32[]{:S(2)}, u32[]{:S(2)}) collective-permute-start(bf16[2,8,32,128]{3,2,1,0:T(8,128)(2,1)S(1)} %collective-permute-done.13.r2), channel_id=1, source_target_pairs={{0,64},{32,96},{64,128},{96,160},{128,192},{160,224},{192,0},{224,... | collective-permute-start | bytes 393224 | tf_op jit(solution)/shard_map/ppermute | solution.py:441
  127.6 17.8 %collective-permute-start.18 = (bf16[2,8,32,128]{3,2,1,0:T(8,128)(2,1)S(1)}, bf16[2,8,32,128]{3,2,1,0:T(8,128)(2,1)S(1)}, u32[]{:S(2)}, u32[]{:S(2)}) collective-permute-start(bf16[2,8,32,128]{3,2,1,0:T(8,128)(2,1)S(1)} %collective-permute-done.17.l2), channel_id=1, source_target_pairs={{0,224},{32,0},{64,32},{96,64},{128,96},{160,128},{192,160},{224,1... | collective-permute-start | bytes 393224 | tf_op jit(solution)/shard_map/ppermute | solution.py:441
  148.1 13.6 %collective-permute-start.19 = (bf16[512,512]{1,0:T(8,128)(2,1)S(1)}, bf16[512,512]{1,0:T(8,128)(2,1)S(1)}, u32[]{:S(2)}, u32[]{:S(2)}) collective-permute-start(bf16[512,512]{1,0:T(8,128)(2,1)S(1)} %get-tuple-element.28), channel_id=1, source_target_pairs={{0,16},{16,0},{1,17},{17,1},{2,18},{18,2},{3,19},{19,3},{4,20},{20... | collective-permute-start | bytes 1572872 | tf_op jit(solution)/shard_map/ppermute | solution.py:411
  (4 other events, 88.5 us)
